TPU v7x, 32 devices: a whole 2x2x4 slice. The times are simulated.
32 devices in a mesh: dp: 32 (over z, y, x, core).
Axes of the slice: x: 2, y: 2, z: 4, core: 2. Of those that a mesh axis runs over, the one named last changes fastest.
Arguments:
- tokens: bfloat16 [128, 512, 576], P('dp'), may hold values from -6 to 6
- doc_starts: int32 [128, 512], P('dp'), may hold values from 0 to 512, as said below
- cotangent: bfloat16 [128, 512, 576], P('dp'), may hold values from -6 to 6
- master: float32 [3543040], P('dp'), may hold values from -2 to 2
- moment_one: float32 [3543040], P('dp'), may hold values from -0.0003 to 0.0003
- moment_two: float32 [3543040], P('dp'), may hold values from 3e-11 to 3e-09
Outputs:
- layer_out: bfloat16 [128, 512, 576], P('dp')
- input_grad: float32 [128, 512, 576], P('dp')
- grad_params: float32 [3543040], P('dp')
- grad_norm: float32 [], replicated
- new_master: float32 [3543040], P('dp')
- new_one: float32 [3543040], P('dp')
- new_two: float32 [3543040], P('dp')
Inputs may be any that keep to these rules, and one draw needn't show every extreme that they name: `doc_starts`: each buffer holds whole documents from its first slot on, then padding in whole tiles of 128 slots; a device's last buffer may be all padding, every other buffer is at least half live; buffer 0 is one document of 512 tokens and buffer 128 - 1 is half padding.
All inputs are finite; a program needn't handle non-finite values.
Results may differ from a plain program's by a relative error of at most 0.012.
The roundings to bfloat16 on the way count: a program that leaves them out, or rounds other values in their place, can miss the bound.
Values may be sent and summed in bfloat16 or wider, within the bound.
No kernel may reach another device: no remote copies, remote signals or barrier semaphores. Data moves between devices by JAX's collectives and lax.ppermute only.
A program may use at most 256 MiB of HBM per device.

v0:
```python
import jax
import jax.numpy as jnp
from jax import lax
from jax.sharding import PartitionSpec as P

MODEL_WIDTH = 576
QUERY_HEADS = 9
KEY_VALUE_HEADS = 3
HEAD_SIZE = 64
FEEDFWD_UNITS = 1536
ROWBLK = 512
STEP = 8


rms_eps = 1e-05
rope_base = 100000.0
learn_rate = 0.02
decay_one = 0.9
decay_two = 0.999
adam_eps = 1e-08
weight_decay = 0.1
clip_norm = 1.0
mask_fill = -1000000000.0


def inner_first(former, latter):
    return lax.dot_general(
        former, latter, (((0,), (0,)), ((), ())), preferred_element_type=jnp.float32
    )


def inner_last(former, latter):
    return lax.dot_general(
        former, latter, (((1,), (1,)), ((), ())), preferred_element_type=jnp.float32
    )


def simple_product(former, latter):
    return jnp.dot(former, latter, preferred_element_type=jnp.float32)


def unpack(flat_params):
    query_width = QUERY_HEADS * HEAD_SIZE
    value_total_width = KEY_VALUE_HEADS * HEAD_SIZE
    layout = [
        (MODEL_WIDTH, query_width),
        (MODEL_WIDTH, value_total_width),
        (MODEL_WIDTH, value_total_width),
        (query_width, MODEL_WIDTH),
        (MODEL_WIDTH, FEEDFWD_UNITS),
        (MODEL_WIDTH, FEEDFWD_UNITS),
        (FEEDFWD_UNITS, MODEL_WIDTH),
        (2, MODEL_WIDTH),
    ]
    pieces = []
    offset = 0
    for height, breadth in layout:
        pieces.append(flat_params[offset : offset + height * breadth].reshape(height, breadth))
        offset = offset + height * breadth
    return pieces


def wide_tables(positions, breadth):
    half_dim = HEAD_SIZE // 2
    column = jnp.arange(breadth) % HEAD_SIZE % half_dim
    frequency = rope_base ** (-(column.astype(jnp.float32) * 2.0 / HEAD_SIZE))
    angles = positions.astype(jnp.float32)[:, None] * frequency[None, :]
    return (jnp.cos(angles), jnp.sin(angles))


def turn_matrix(breadth):
    half_dim = HEAD_SIZE // 2
    rows_at = jnp.arange(breadth)[:, None]
    cols_at = jnp.arange(breadth)[None, :]
    within = cols_at % HEAD_SIZE
    minus = (within < half_dim) & (rows_at == cols_at + half_dim)
    plus = (within >= half_dim) & (rows_at == cols_at - half_dim)
    return jnp.where(minus, -1.0, jnp.where(plus, 1.0, 0.0)).astype(jnp.float32)


def turn_rows(values, turner):
    return jnp.dot(values, turner, precision=lax.Precision.HIGHEST)


def apply_rotary(values, cosine_lookup, sine_lookup, turner):
    return values * cosine_lookup + turn_rows(values, turner) * sine_lookup


def rotate_back(grad_rows, cosine_lookup, sine_lookup, turner):
    return grad_rows * cosine_lookup - turn_rows(grad_rows * sine_lookup, turner)


def norm_forward(values, gain_row):
    inverse = lax.rsqrt(jnp.mean(values * values, axis=-1, keepdims=True) + rms_eps)
    return (values * inverse * gain_row, inverse)


def norm_backward(values, inverse, gain_row, grad_rows):
    weighted = grad_rows * gain_row
    gain_grad = jnp.sum(grad_rows * values * inverse, axis=0)
    input_grad = inverse * weighted - values * inverse**3 * jnp.mean(
        weighted * values, axis=-1, keepdims=True
    )
    return (input_grad, gain_grad)


def block_scores(rotated_query, rotated_key, starts, row_start, row_end):
    token_index = jnp.arange(row_end)
    scores = jnp.einsum(
        "qgcd,kgd->gcqk", rotated_query, rotated_key, preferred_element_type=jnp.float32
    ) * HEAD_SIZE ** (-0.5)
    allowed = (starts[row_start:row_end, None] == starts[None, :row_end]) & (
        token_index[row_start:row_end, None] >= token_index[None, :]
    )
    return jnp.where(allowed[None, None], scores, mask_fill)


def attend(rotated_query, rotated_key, value_lower, starts):
    sequence_length = rotated_query.shape[0]
    block_rows = min(ROWBLK, sequence_length)
    scores = block_scores(rotated_query, rotated_key, starts, 0, block_rows)
    row_peak = jnp.max(scores, axis=-1, keepdims=True)
    log_total = row_peak + jnp.log(jnp.sum(jnp.exp(scores - row_peak), axis=-1, keepdims=True))
    prob_low = jnp.exp(scores - log_total).astype(jnp.bfloat16)
    outputs = jnp.einsum(
        "gcqk,kgd->qgcd", prob_low, value_lower, preferred_element_type=jnp.float32
    )
    row_totals = [log_total]
    return (outputs, row_totals)


def attend_back(rotated_query, rotated_key, value_lower, starts, row_totals, mixed_grad):
    sequence_length = rotated_query.shape[0]
    block_rows = min(ROWBLK, sequence_length)
    score_scale = HEAD_SIZE ** (-0.5)
    query_grads = []
    key_grad = jnp.zeros(rotated_key.shape, jnp.float32)
    value_gradient = jnp.zeros(value_lower.shape, jnp.float32)
    for block_index, row_start in enumerate(range(0, sequence_length, block_rows)):
        row_end = row_start + block_rows
        scores = block_scores(rotated_query, rotated_key, starts, row_start, row_end)
        prob_full = jnp.exp(scores - row_totals[block_index])
        prob_grad = jnp.einsum(
            "qgcd,kgd->gcqk", mixed_grad, value_lower, preferred_element_type=jnp.float32
        )
        score_low = (
            prob_full * (prob_grad - jnp.sum(prob_full * prob_grad, axis=-1, keepdims=True))
        ).astype(jnp.bfloat16)
        query_grads.append(
            jnp.einsum("gcqk,kgd->qgcd", score_low, rotated_key, preferred_element_type=jnp.float32)
            * score_scale
        )
        key_grad = key_grad.at[:row_end].add(
            jnp.einsum(
                "gcqk,qgcd->kgd", score_low, rotated_query, preferred_element_type=jnp.float32
            )
            * score_scale
        )
        value_gradient = value_gradient.at[:row_end].add(
            jnp.einsum(
                "gcqk,qgcd->kgd",
                prob_full.astype(jnp.bfloat16),
                mixed_grad,
                preferred_element_type=jnp.float32,
            )
        )
    return (query_grads[0], key_grad, value_gradient)


def flatten_grads(grad_pieces):
    return jnp.concatenate([piece.reshape(-1) for piece in grad_pieces])


def local(tokens, doc_starts, cotangent, master, moment_one, moment_two):
    buffers = tokens.shape[0]
    sequence_length = tokens.shape[1]
    whole_rows = master.shape[0] * lax.axis_size("dp")
    parameter_count = (
        2 * MODEL_WIDTH * QUERY_HEADS * HEAD_SIZE
        + 2 * MODEL_WIDTH * KEY_VALUE_HEADS * HEAD_SIZE
        + 3 * MODEL_WIDTH * FEEDFWD_UNITS
        + 2 * MODEL_WIDTH
    )
    heads_per_group = QUERY_HEADS // KEY_VALUE_HEADS
    query_width = QUERY_HEADS * HEAD_SIZE
    value_total_width = KEY_VALUE_HEADS * HEAD_SIZE
    query_turner = turn_matrix(query_width)
    key_turner = turn_matrix(value_total_width)
    master_low = master.astype(jnp.bfloat16)
    grad_parts = None
    token_index = jnp.arange(sequence_length)
    layer_rows = []
    input_rows = []
    for buffer_index in range(buffers):
        forward_flat = lax.all_gather(master_low, "dp", axis=0, tiled=True)
        (
            query_weight,
            key_matrix,
            value_matrix,
            output_weight,
            gate_weight,
            up_weight,
            down_weight,
            norm_gains,
        ) = unpack(forward_flat)
        gain_one = norm_gains[0].astype(jnp.float32)
        gain_two = norm_gains[1].astype(jnp.float32)
        values_in = tokens[buffer_index].astype(jnp.float32)
        starts = doc_starts[buffer_index]
        live_rows = (starts < sequence_length).astype(jnp.float32)[:, None]
        positions = jnp.where(starts < sequence_length, token_index - starts, 0)
        cosine_query, sine_query = wide_tables(positions, query_width)
        cosine_key, sine_key = wide_tables(positions, value_total_width)
        first_normalized, inverse_one = norm_forward(values_in, gain_one)
        normalized_lower = first_normalized.astype(jnp.bfloat16)
        rotated_query = apply_rotary(
            simple_product(normalized_lower, query_weight), cosine_query, sine_query, query_turner
        ).astype(jnp.bfloat16)
        rotated_key = apply_rotary(
            simple_product(normalized_lower, key_matrix), cosine_key, sine_key, key_turner
        ).astype(jnp.bfloat16)
        value_lower = (
            simple_product(normalized_lower, value_matrix)
            .astype(jnp.bfloat16)
            .reshape(sequence_length, KEY_VALUE_HEADS, HEAD_SIZE)
        )
        grouped_heads = rotated_query.reshape(
            sequence_length, KEY_VALUE_HEADS, heads_per_group, HEAD_SIZE
        )
        key_heads = rotated_key.reshape(sequence_length, KEY_VALUE_HEADS, HEAD_SIZE)
        mixed, row_totals = attend(grouped_heads, key_heads, value_lower, starts)
        mixed_low = mixed.reshape(sequence_length, query_width).astype(jnp.bfloat16)
        hidden = values_in + simple_product(mixed_low, output_weight)
        normed_two, inverse_two = norm_forward(hidden, gain_two)
        normed_two_low = normed_two.astype(jnp.bfloat16)
        gate_pre = simple_product(normed_two_low, gate_weight)
        up_pre = simple_product(normed_two_low, up_weight)
        activated = (jax.nn.silu(gate_pre) * up_pre).astype(jnp.bfloat16)
        result = hidden + simple_product(activated, down_weight)
        layer_rows.append((result * live_rows).astype(jnp.bfloat16))
        backward_flat = lax.all_gather(master_low, "dp", axis=0, tiled=True)
        (
            query_weight,
            key_matrix,
            value_matrix,
            output_weight,
            gate_weight,
            up_weight,
            down_weight,
            norm_gains,
        ) = unpack(backward_flat)
        result_grad = cotangent[buffer_index].astype(jnp.float32) * live_rows
        result_low = result_grad.astype(jnp.bfloat16)
        down_grad = inner_first(activated, result_low)
        act_grad = inner_last(result_low, down_weight)
        gate_sigmoid = jax.nn.sigmoid(gate_pre)
        gate_low = (
            act_grad * up_pre * gate_sigmoid * (1.0 + gate_pre * (1.0 - gate_sigmoid))
        ).astype(jnp.bfloat16)
        up_low = (act_grad * gate_pre * gate_sigmoid).astype(jnp.bfloat16)
        gate_grad = inner_first(normed_two_low, gate_low)
        up_grad = inner_first(normed_two_low, up_low)
        normed_two_grad = inner_last(gate_low, gate_weight) + inner_last(up_low, up_weight)
        hidden_norm_grad, gain_two_grad = norm_backward(
            hidden, inverse_two, gain_two, normed_two_grad
        )
        hidden_grad = result_grad + hidden_norm_grad
        hidden_low = hidden_grad.astype(jnp.bfloat16)
        output_grad = inner_first(mixed_low, hidden_low)
        mixed_grad = (
            inner_last(hidden_low, output_weight)
            .astype(jnp.bfloat16)
            .reshape(sequence_length, KEY_VALUE_HEADS, heads_per_group, HEAD_SIZE)
        )
        query_rot_grad, key_rot_grad, value_gradient = attend_back(
            grouped_heads, key_heads, value_lower, starts, row_totals, mixed_grad
        )
        query_low = rotate_back(
            query_rot_grad.reshape(sequence_length, query_width),
            cosine_query,
            sine_query,
            query_turner,
        ).astype(jnp.bfloat16)
        key_low = rotate_back(
            key_rot_grad.reshape(sequence_length, value_total_width),
            cosine_key,
            sine_key,
            key_turner,
        ).astype(jnp.bfloat16)
        value_gradient_lower = value_gradient.reshape(sequence_length, value_total_width).astype(
            jnp.bfloat16
        )
        query_grad = inner_first(normalized_lower, query_low)
        key_grad = inner_first(normalized_lower, key_low)
        value_weight_grad = inner_first(normalized_lower, value_gradient_lower)
        normed_one_grad = (
            inner_last(query_low, query_weight)
            + inner_last(key_low, key_matrix)
            + inner_last(value_gradient_lower, value_matrix)
        )
        input_norm_grad, gain_one_grad = norm_backward(
            values_in, inverse_one, gain_one, normed_one_grad
        )
        input_rows.append(hidden_grad + input_norm_grad)
        grad_pieces = (
            query_grad,
            key_grad,
            value_weight_grad,
            output_grad,
            gate_grad,
            up_grad,
            down_grad,
            gain_one_grad,
            gain_two_grad,
        )
        if grad_parts is None:
            grad_parts = grad_pieces
        else:
            grad_parts = tuple((total + piece for total, piece in zip(grad_parts, grad_pieces)))
    grad_shard = lax.psum_scatter(
        jnp.pad(flatten_grads(grad_parts), (0, whole_rows - parameter_count)),
        "dp",
        scatter_dimension=0,
        tiled=True,
    )
    square_sum = lax.psum(jnp.sum(grad_shard * grad_shard), "dp")
    grad_norm = jnp.sqrt(square_sum)
    clipped = grad_shard * (clip_norm / jnp.maximum(grad_norm, clip_norm))
    new_one = decay_one * moment_one + (1.0 - decay_one) * clipped
    new_two = decay_two * moment_two + (1.0 - decay_two) * clipped * clipped
    corrected_one = new_one / (1.0 - decay_one**STEP)
    corrected_two = new_two / (1.0 - decay_two**STEP)
    new_master = master - learn_rate * (
        corrected_one / (jnp.sqrt(corrected_two) + adam_eps) + weight_decay * master
    )
    return (
        jnp.stack(layer_rows),
        jnp.stack(input_rows),
        grad_shard,
        grad_norm,
        new_master,
        new_one,
        new_two,
    )


def solution(mesh):
    placed = (P("dp", None, None), P("dp", None), P("dp", None, None), P("dp"), P("dp"), P("dp"))
    return jax.shard_map(
        local,
        mesh=mesh,
        in_specs=placed,
        out_specs=(
            P("dp", None, None),
            P("dp", None, None),
            P("dp"),
            P(),
            P("dp"),
            P("dp"),
            P("dp"),
        ),
        check_vma=False,
    )
```

profile of v0, /device:TPU:0, one launch (start us, length us, event | category | flops | bytes accessed | tf_op | source)
XLA Modules:
  0.0 1200.8 jit_solution(10160810566967421815)
XLA Ops:
  16.3 101.2 %all-gather.3.cloned.1.call-done = bf16[32,1,110720]{2,1,0:T(2,128)(2,1)} async-done(((bf16[1,1,110720]{2,1,0:T(2,128)(2,1)}), bf16[32,1,110720]{2,1,0:T(2,128)(2,1)}) %all-gather.3.cloned.1.call-update) | async-done | bytes 7086096 | tf_op jit(solution)/shard_map/all_gather | solution.py:195
  117.5 151.1 %reduce.16 = bf16[32,110720]{1,0:T(8,128)(2,1)} reduce(bf16[32,1,110720]{2,1,0:T(2,128)(2,1)} %all-gather.3.cloned.1.call-done, bf16[]{:T(256)} %constant.429), dimensions={1}, to_apply=%all-gather.reduce_sub_computation | reduce | bytes 14172162 | tf_op jit(solution)/shard_map/all_gather | solution.py:195
  268.6 13.4 %reshape.1319 = bf16[3543040]{0:T(1024)(128)(2,1)} reshape(bf16[32,110720]{1,0:T(8,128)(2,1)} %reduce.16) | data formatting | bytes 14172160
  296.1 3.3 fusion.519
  299.4 3.2 fusion.513
  312.7 3.2 fusion.191
  315.9 7.6 fusion.99
  335.7 7.8 fusion.101
  353.5 4.4 reshape.1279
  357.9 4.8 reshape.1280
  364.9 3.1 fusion.536
  368.0 3.1 fusion.537
  371.1 3.0 fusion.540
  374.1 3.1 fusion.541
  383.5 7.8 fusion.98
  401.3 4.3 reshape.1281
  405.5 7.5 multiply_convert_fusion.6
  416.4 4.0 multiply_convert_fusion.2
  428.9 7.8 fusion.100
  446.9 3.1 fusion.542
  450.0 3.1 fusion.543
  454.5 3.3 fusion.539
  457.8 5.4 multiply_convert_fusion
  464.4 4.8 multiply_convert_fusion.4
  476.1 6.3 fusion.6
  482.4 11.2 fusion.8
  493.6 4.4 convolution_multiply_fusion.2
  498.1 5.1 fusion.119
  503.2 3.2 fusion.195
  507.3 5.6 fusion.9
  512.9 11.3 fusion.11
  524.2 4.4 convolution_multiply_fusion.3
  530.2 6.8 fusion.194
  538.1 5.7 fusion.3
  543.8 11.3 fusion.5
  555.1 4.5 convolution_multiply_fusion.1
  561.9 6.8 fusion.196
  569.7 5.9 fusion
  575.6 11.4 fusion.2
  587.0 3.4 convolution_multiply_fusion
  592.5 6.8 fusion.197
  599.4 11.5 fusion.107
  613.8 11.5 fusion.109
  627.3 11.7 fusion.108
  659.2 3.0 fusion.551
  665.1 3.9 fusion.199
  669.0 3.2 fusion.198
  677.1 3.4 fusion.200
  680.5 11.3 fusion.106
  693.8 3.9 fusion.201
  722.1 4.7 add_add_fusion.3
  729.6 7.5 add_add_fusion.2
  737.1 4.6 reshape.1307
  741.7 7.5 add_add_fusion.1
  749.2 4.8 reshape.1308
  759.7 3.0 add_add_fusion
  762.7 5.3 copy.66
  768.0 5.4 reshape.1309
  773.4 4.6 fusion.167
  778.1 112.5 %concatenate.19 = f32[3540096]{0:T(1024)} concatenate(f32[331776]{0:T(1024)} %reshape.1303, f32[110592]{0:T(1024)S(1)} %copy-done.91, f32[110592]{0:T(1024)} %reshape.1305, f32[331776]{0:T(1024)} %reshape.1306, f32[884736]{0:T(1024)} %reshape.1307, f32[884736]{0:T(1024)} %reshape.1308, f32[884736]{0:T(1024)} %reshape.1309, f32[576]{0:T(1024)S(1)} %add_add_fusion.6, ...), dimensions={0} | concatenate | bytes 28320768 | tf_op jit(solution)/shard_map/concatenate | solution.py:171
  890.6 10.6 pad.28
  901.3 3.6 fusion.110
  918.4 230.7 %all-reduce.4.cloned.1.call-done = f32[3543040]{0:T(1024)} async-done(((f32[3543040]{0:T(1024)}), f32[3543040]{0:T(1024)}) %all-reduce.4.cloned.1.call-update) | async-done | bytes 14172176
  1151.0 39.5 %psum.7 = f32[]{:T(128)} all-reduce(f32[]{:T(128)} %get-tuple-element.196), channel_id=1, replica_groups=mesh['dp'=32] {'dp'}, use_global_device_ids=true, to_apply=%region_38.39 | all-reduce | flops 1 | bytes 8 | tf_op jit(solution)/shard_map/psum | solution.py:326
  (637 shorter events, 197.1 us)
Async XLA Ops:
  7.2 110.3 %all-gather.3.cloned.1.call-start = ((), (), s32[]{:S(2)}) async-start(), calls=%async_computation | async-start | bytes 14615040 | tf_op jit(solution)/shard_map/all_gather | solution.py:195
  9.3 1139.9 %all-reduce.4.cloned.1.call-start = ((), (), s32[]{:S(2)}) async-start(), calls=%async_computation.1 | async-start | bytes 28344320
  9.3 372.1 %copy-start.211 = (f32[192]{0:T(256)}, f32[192]{0:T(256)S(1)}, u32[]{:S(2)}) copy-start(f32[192]{0:T(256)S(1)} %fusion.444) | copy-start | bytes 2308
  9.4 303.3 %copy-start.214 = (pred[192]{0:T(512)(128)(4,1)}, pred[192]{0:T(512)(128)(4,1)S(1)}, u32[]{:S(2)}) copy-start(pred[192]{0:T(512)(128)(4,1)S(1)} %get-tuple-element.287) | copy-start | bytes 580
  9.4 303.3 %copy-start.217 = (pred[192]{0:T(512)(128)(4,1)}, pred[192]{0:T(512)(128)(4,1)S(1)}, u32[]{:S(2)}) copy-start(pred[192]{0:T(512)(128)(4,1)S(1)} %get-tuple-element.288) | copy-start | bytes 580
  9.4 372.0 %copy-start.197 = (s32[192]{0:T(256)}, s32[192]{0:T(256)S(1)}, u32[]{:S(2)}) copy-start(s32[192]{0:T(256)S(1)} %get-tuple-element.285) | copy-start | bytes 2308
  9.4 372.0 %copy-start.200 = (s32[192]{0:T(256)}, s32[192]{0:T(256)S(1)}, u32[]{:S(2)}) copy-start(s32[192]{0:T(256)S(1)} %get-tuple-element.286) | copy-start | bytes 2308
  9.4 374.0 %copy-start.203 = (pred[576]{0:T(1024)(128)(4,1)}, pred[576]{0:T(1024)(128)(4,1)S(1)}, u32[]{:S(2)}) copy-start(pred[576]{0:T(1024)(128)(4,1)S(1)} %get-tuple-element.291) | copy-start | bytes 1732
  9.4 374.0 %copy-start.206 = (pred[576]{0:T(1024)(128)(4,1)}, pred[576]{0:T(1024)(128)(4,1)S(1)}, u32[]{:S(2)}) copy-start(pred[576]{0:T(1024)(128)(4,1)S(1)} %get-tuple-element.292) | copy-start | bytes 1732
  9.5 374.0 %copy-start.179 = (f32[576]{0:T(1024)}, f32[576]{0:T(1024)S(1)}, u32[]{:S(2)}) copy-start(f32[576]{0:T(1024)S(1)} %fusion.435) | copy-start | bytes 6916
  9.5 374.0 %copy-start.182 = (s32[576]{0:T(1024)}, s32[576]{0:T(1024)S(1)}, u32[]{:S(2)}) copy-start(s32[576]{0:T(1024)S(1)} %get-tuple-element.289) | copy-start | bytes 6916
  9.5 374.0 %copy-start.185 = (s32[576]{0:T(1024)}, s32[576]{0:T(1024)S(1)}, u32[]{:S(2)}) copy-start(s32[576]{0:T(1024)S(1)} %get-tuple-element.290) | copy-start | bytes 6916
  11.6 371.9 %copy-start.189 = (f32[512]{0:T(512)}, f32[512]{0:T(512)S(1)}, u32[]{:S(2)}) copy-start(f32[512]{0:T(512)S(1)} %select_convert_fusion) | copy-start | bytes 6148
  11.6 304.3 %copy-start.191 = (f32[512]{0:T(512)}, f32[512]{0:T(512)S(1)}, u32[]{:S(2)}) copy-start(f32[512]{0:T(512)S(1)} %select_convert_fusion.1) | copy-start | bytes 6148
  11.7 324.0 %copy-start.193 = (f32[512]{0:T(512)}, f32[512]{0:T(512)S(1)}, u32[]{:S(2)}) copy-start(f32[512]{0:T(512)S(1)} %select_convert_fusion.3) | copy-start | bytes 6148
  12.3 401.9 %copy-start.154 = (f32[512]{0:T(512)}, f32[512]{0:T(512)S(1)}, u32[]{:S(2)}) copy-start(f32[512]{0:T(512)S(1)} %get-tuple-element.294) | copy-start | bytes 6148
  12.3 431.4 %copy-start.152 = (f32[512]{0:T(512)}, f32[512]{0:T(512)S(1)}, u32[]{:S(2)}) copy-start(f32[512]{0:T(512)S(1)} %get-tuple-element.293) | copy-start | bytes 6148
  13.5 282.6 %copy-start.158 = (f32[512]{0:T(512)}, f32[512]{0:T(512)S(1)}, u32[]{:S(2)}) copy-start(f32[512]{0:T(512)S(1)} %get-tuple-element.245) | copy-start | bytes 6148
  13.5 285.9 %copy-start.160 = (f32[512]{0:T(512)}, f32[512]{0:T(512)S(1)}, u32[]{:S(2)}) copy-start(f32[512]{0:T(512)S(1)} %get-tuple-element.281) | copy-start | bytes 6148
  14.1 291.9 %copy-start.164 = (f32[512]{0:T(512)}, f32[512]{0:T(512)S(1)}, u32[]{:S(2)}) copy-start(f32[512]{0:T(512)S(1)} %get-tuple-element.283) | copy-start | bytes 6148
  14.1 365.6 %copy-start.162 = (f32[512]{0:T(512)}, f32[512]{0:T(512)S(1)}, u32[]{:S(2)}) copy-start(f32[512]{0:T(512)S(1)} %get-tuple-element.241) | copy-start | bytes 6148
  14.5 313.1 %copy-start.8 = (pred[512,512]{0,1:T(8,128)(4,1)}, pred[512,512]{0,1:T(8,128)(4,1)S(1)}, u32[]{:S(2)}) copy-start(pred[512,512]{0,1:T(8,128)(4,1)S(1)} %fusion.203) | copy-start | bytes 786436
  283.9 95.8 %copy-start.138 = (f32[576]{0:T(1024)}, f32[576]{0:T(1024)S(1)}, u32[]{:S(2)}) copy-start(f32[576]{0:T(1024)S(1)} %get-tuple-element.202) | copy-start | bytes 6916
  293.4 14.3 %slice-start.9 = ((s8[7086080]{0:T(1024)(128)(4,1)}), s8[2891776]{0:T(1024)(128)(4,1)S(1)}, s32[]{:S(2)}) async-start(s8[7086080]{0:T(1024)(128)(4,1)} %bitcast.654), calls=%async_computation.11 | async-start | bytes 5783552
  296.1 8.6 copy-start.53
  299.4 8.3 slice-start.10
  315.9 7.7 copy-start.115
  335.7 7.8 copy-start.10
  364.8 9.4 copy-start.50
  383.5 7.8 copy-start.117
  405.5 7.5 copy-start.93
  405.5 8.6 copy-start.226
  405.5 8.6 copy-start.227
  413.0 8.5 copy-start.96
  428.9 7.8 copy-start.11
  438.3 37.8 %copy-start.3 = (f32[3,512,512,3]{2,1,3,0:T(8,128)}, f32[3,512,512,3]{2,1,3,0:T(8,128)S(1)}, u32[]{:S(2)}) copy-start(f32[3,512,512,3]{2,1,3,0:T(8,128)S(1)} %get-tuple-element.266) | copy-start | bytes 28311556
  440.3 35.8 %copy-start.136 = (f32[3,3,512]{2,1,0:T(4,128)}, f32[3,3,512]{2,1,0:T(4,128)S(1)}, u32[]{:S(2)}) copy-start(f32[3,3,512]{2,1,0:T(4,128)S(1)} %log_add_fusion.2) | copy-start | bytes 55300
  443.6 30.1 %copy-start.40 = (f32[512,576]{0,1:T(8,128)}, f32[512,576]{0,1:T(8,128)S(1)}, u32[]{:S(2)}) copy-start(f32[512,576]{0,1:T(8,128)S(1)} %get-tuple-element.268) | copy-start | bytes 3538948
  446.9 7.6 copy-start.46
  463.2 7.2 copy-start.109
  475.5 6.9 copy-start.21
  493.6 9.5 copy-start.4
  493.6 9.5 copy-start.75
  493.6 9.5 copy-start.137
  498.1 8.9 slice-start.6
  528.6 9.1 slice-start
  530.2 6.9 copy-start.15
  530.2 6.9 copy-start.33
  530.2 7.5 slice-start.1
  530.2 7.5 slice-start.2
  543.7 11.3 copy-start.116
  559.6 9.8 slice-start.3
  561.9 6.9 copy-start.24
  561.9 6.9 copy-start.34
  561.9 7.5 slice-start.4
  561.9 7.5 slice-start.5
  575.6 11.4 copy-start.118
  592.4 6.9 copy-start.114
  592.4 6.9 copy-start.181
  599.3 11.5 copy-start.28
  915.7 275.5 %copy-start.89 = (f32[110720]{0:T(1024)S(1)}, f32[110720]{0:T(1024)}, u32[]{:S(2)}) copy-start(f32[110720]{0:T(1024)} %param.41) | copy-start | bytes 1328644
  915.7 275.5 %copy-start.126 = (f32[110720]{0:T(1024)S(1)}, f32[110720]{0:T(1024)}, u32[]{:S(2)}) copy-start(f32[110720]{0:T(1024)} %param.42) | copy-start | bytes 1328644
  915.7 275.5 %copy-start.127 = (f32[110720]{0:T(1024)S(1)}, f32[110720]{0:T(1024)}, u32[]{:S(2)}) copy-start(f32[110720]{0:T(1024)} %param.43) | copy-start | bytes 1328644
  1151.0 41.6 %copy-start.90 = (f32[110720]{0:T(1024)}, f32[110720]{0:T(1024)S(1)}, u32[]{:S(2)}) copy-start(f32[110720]{0:T(1024)S(1)} %get-tuple-element.197) | copy-start | bytes 1328644
  (180 other events, 509.3 us)
Sparse Core Ops, SparseCore 0:
  11.5 105.9 all-gather.2
  901.4 247.7 all-reduce.3
where the time goes:
time: 1210 us; the launch traced here: 1200 us
  matrix products  365 us (30%)
  waiting for transfers between devices  332 us (27%)
  other arithmetic  230 us (19%)
  local copies, waits for them, and re-layouts  216 us (18%)
  blocking collectives  39.5 us (3%)
  between operations  18.6 us (2%)
    unnamed x3, waiting for transfers between devices  231 us
    all_gather x1, other arithmetic, local(): forward_flat = lax.all_gather(master_low, 'dp', axis=0, tiled=True)  151 us
    concatenate x1, local copies, waits for them, and re-layouts, flatten_grads(): return jnp.concatenate([piece.reshape(-1) for piece in grad_pieces])  112 us
    all_gather x1, waiting for transfers between devices, local(): forward_flat = lax.all_gather(master_low, 'dp', axis=0, tiled=True)  101 us
    dot_general x16, matrix products, turn_rows(): return jnp.dot(values, turner, precision=lax.Precision.HIGHEST)  101 us
    dot_general x28, matrix products, inner_first(): lax.dot_general(former, latter, (((0,), (0,)), ((), ())), preferred_eleme...  59.8 us
    dot_general x28, matrix products, simple_product(): return jnp.dot(former, latter, preferred_element_type=jnp.float32)  58.1 us
    dot_general x28, matrix products, inner_last(): lax.dot_general(former, latter, (((1,), (1,)), ((), ())), preferred_eleme...  56.7 us
  transfers between devices with their start and end apart: 2, of which 2 were waited for; matrix products, arithmetic and copies ran while one was open for 2% of the time, Pallas kernels for 0%

commit v1 on v0

v1 whole, which is shorter than its diff:
```python
import functools

import jax
import jax.numpy as jnp
from jax import lax
from jax.experimental import pallas as pl
from jax.experimental.pallas import tpu as pltpu
from jax.sharding import PartitionSpec as P

MODEL_WIDTH = 576
QUERY_HEADS = 9
KEY_VALUE_HEADS = 3
HEAD_SIZE = 64
FEEDFWD_UNITS = 1536
TILE = 128
STEP = 8
GROUP = QUERY_HEADS // KEY_VALUE_HEADS
HALF = HEAD_SIZE // 2
KV_WIDTH = KEY_VALUE_HEADS * HEAD_SIZE
QKV_WIDTH = MODEL_WIDTH + 2 * KV_WIDTH
CHUNK = 512

rms_eps = 1e-05
rope_base = 100000.0
learn_rate = 0.02
decay_one = 0.9
decay_two = 0.999
adam_eps = 1e-08
weight_decay = 0.1
clip_norm = 1.0
mask_fill = -1000000000.0

bf16 = jnp.bfloat16
f32 = jnp.float32


def mm(a, b):
    return jnp.dot(a, b, preferred_element_type=f32)


def inverse_rms(x):
    return lax.rsqrt(jnp.mean(x * x, axis=-1, keepdims=True) + rms_eps)


def fill_bias(bias, starts_col, starts_row):
    rows = starts_col.shape[0]
    key_at = lax.broadcasted_iota(jnp.int32, (rows, TILE), 0)
    for i in range(rows // TILE):
        width = (i + 1) * TILE
        query_at = lax.broadcasted_iota(jnp.int32, (rows, TILE), 1) + i * TILE
        allowed = (starts_col == starts_row[:, i * TILE : width]) & (key_at <= query_at)
        bias[:, i * TILE : width] = jnp.where(allowed, 0.0, mask_fill)


def head_rows(ref, g, columns):
    return jnp.concatenate(
        [ref[0, pl.ds((g * GROUP + h) * HEAD_SIZE, HEAD_SIZE), columns] for h in range(GROUP)], axis=1
    )


def attention_forward(
    live, tok, st_row, st_col, cos, sin, wq, wk, wv, wo, gain, qk_t, kv, mix_t, hidden, lse, w_t, v_t, bias
):
    b = pl.program_id(0)
    rows = tok.shape[1]

    @pl.when(b == 0)
    def _():
        w_t[0:MODEL_WIDTH] = wq[...].T
        w_t[MODEL_WIDTH : MODEL_WIDTH + KV_WIDTH] = wk[...].T
        w_t[MODEL_WIDTH + KV_WIDTH : QKV_WIDTH] = wv[...].T

    @pl.when(live[b] > 0)
    def _():
        x = tok[0].astype(f32)
        n1_t = (x * inverse_rms(x) * gain[...]).astype(bf16).T
        c, s = cos[0], sin[0]
        for h in range(QUERY_HEADS + KEY_VALUE_HEADS):
            at = h * HEAD_SIZE
            u = mm(w_t[at : at + HEAD_SIZE], n1_t)
            u1, u2 = u[:HALF], u[HALF:]
            r = jnp.concatenate([u1 * c - u2 * s, u2 * c + u1 * s], axis=0)
            if h < QUERY_HEADS:
                r = r * HEAD_SIZE ** (-0.5)
            r = r.astype(bf16)
            qk_t[0, at : at + HEAD_SIZE] = r
            if h >= QUERY_HEADS:
                kv[0, h - QUERY_HEADS] = r.T
        for g in range(KEY_VALUE_HEADS):
            at = MODEL_WIDTH + KV_WIDTH + g * HEAD_SIZE
            v = mm(w_t[at : at + HEAD_SIZE], n1_t).astype(bf16)
            v_t[g] = v
            kv[0, KEY_VALUE_HEADS + g] = v.T
        fill_bias(bias, st_col[0], st_row[0])
        mix_t[...] = jnp.zeros_like(mix_t)

        def group(g, carry):
            for i in range(rows // TILE):

                @pl.when(i < live[b])
                def _():
                    width = (i + 1) * TILE
                    cols = slice(i * TILE, width)
                    q_t = head_rows(qk_t, g, cols)
                    mask = bias[:width, cols]
                    scores = mm(kv[0, g, :width], q_t) + jnp.concatenate([mask] * GROUP, axis=1)
                    peak = jnp.max(scores, axis=0, keepdims=True)
                    e = jnp.exp(scores - peak)
                    total = jnp.sum(e, axis=0, keepdims=True)
                    prob = (e * (1.0 / total)).astype(bf16)
                    lse[0, g * (rows // TILE) + i] = peak + jnp.log(total)
                    out = mm(v_t[g, :, :width], prob).astype(bf16)
                    for h in range(GROUP):
                        mix_t[0, pl.ds((g * GROUP + h) * HEAD_SIZE, HEAD_SIZE), cols] = out[
                            :, h * TILE : (h + 1) * TILE
                        ]

            return carry

        lax.fori_loop(0, KEY_VALUE_HEADS, group, 0)
        hidden[0] = x + mm(mix_t[0].T, wo[...])


def mlp(
    live, hidden, cot, st_col, wg, wu, wd, gain, layer, hgrad, dwg, dwu, dwd_t, dgain,
    wg_t, wu_t, wd_t, n2, n2_t, rl, rl_t, n2g, res
):
    b = pl.program_id(0)
    rows = hidden.shape[1]

    @pl.when(b == 0)
    def _():
        wg_t[...] = wg[...].T
        wu_t[...] = wu[...].T
        wd_t[...] = wd[...].T
        dwg[...] = jnp.zeros_like(dwg)
        dwu[...] = jnp.zeros_like(dwu)
        dwd_t[...] = jnp.zeros_like(dwd_t)
        dgain[...] = jnp.zeros_like(dgain)

    @pl.when(live[b] == 0)
    def _():
        layer[...] = jnp.zeros_like(layer)
        hgrad[...] = jnp.zeros_like(hgrad)

    @pl.when(live[b] > 0)
    def _():
        x = hidden[0]
        inverse = inverse_rms(x)
        alive = st_col[0] < rows
        normed = (x * inverse * gain[...]).astype(bf16)
        n2[...] = normed
        n2_t[...] = normed.T
        grad = jnp.where(alive, cot[0].astype(f32), 0.0).astype(bf16)
        rl[...] = grad
        rl_t[...] = grad.T
        res[...] = jnp.zeros_like(res)
        n2g[...] = jnp.zeros_like(n2g)

        def chunk(k, carry):
            at = pl.ds(pl.multiple_of(k * CHUNK, CHUNK), CHUNK)
            pre = mm(n2[...], wg[:, at])
            up = mm(n2[...], wu[:, at])
            ag = mm(rl[...], wd_t[:, at])
            s = jax.nn.sigmoid(pre)
            silu = pre * s
            act = (silu * up).astype(bf16)
            gl = (ag * up * s * (1.0 + pre * (1.0 - s))).astype(bf16)
            ul = (ag * silu).astype(bf16)
            res[...] += mm(act, wd[at, :])
            n2g[...] += mm(gl, wg_t[at, :]) + mm(ul, wu_t[at, :])
            dwd_t[:, at] += mm(rl_t[...], act)
            dwg[:, at] += mm(n2_t[...], gl)
            dwu[:, at] += mm(n2_t[...], ul)
            return carry

        lax.fori_loop(0, FEEDFWD_UNITS // CHUNK, chunk, 0)
        x = hidden[0]
        layer[0] = jnp.where(alive, x + res[...], 0.0).astype(bf16)
        ng = n2g[...]
        dgain[...] += jnp.sum(ng * x * inverse, axis=0, keepdims=True)
        e = ng * gain[...]
        hgrad[0] = (
            rl[...].astype(f32)
            + inverse * e
            - x * (inverse * inverse * inverse) * jnp.mean(e * x, axis=-1, keepdims=True)
        )


def attention_backward(
    live, hgrad, tok, qk_t, kv, mix_t, lse, st_row, st_col, cos, sin, wq, wk, wv, wo, gain,
    igrad, dw_t, dwo, dgain, w, bias, mg_t, mg, q, dq, dk, dv, low_t
):
    b = pl.program_id(0)
    rows = tok.shape[1]
    tiles = rows // TILE
    scale = HEAD_SIZE ** (-0.5)

    @pl.when(b == 0)
    def _():
        w[:, 0:MODEL_WIDTH] = wq[...]
        w[:, MODEL_WIDTH : MODEL_WIDTH + KV_WIDTH] = wk[...]
        w[:, MODEL_WIDTH + KV_WIDTH : QKV_WIDTH] = wv[...]
        dw_t[...] = jnp.zeros_like(dw_t)
        dwo[...] = jnp.zeros_like(dwo)
        dgain[...] = jnp.zeros_like(dgain)

    @pl.when(live[b] == 0)
    def _():
        igrad[...] = jnp.zeros_like(igrad)

    @pl.when(live[b] > 0)
    def _():
        hl = hgrad[0].astype(bf16)
        dwo[...] += mm(mix_t[0], hl)
        mg_t[0] = mm(wo[...], hl.T).astype(bf16)
        for h in range(QUERY_HEADS):
            at = slice(h * HEAD_SIZE, (h + 1) * HEAD_SIZE)
            mg[h] = mg_t[0, at].T
            q[h] = qk_t[0, at].T
        fill_bias(bias, st_col[0], st_row[0])
        dq[...] = jnp.zeros_like(dq)
        dk[...] = jnp.zeros_like(dk)
        dv[...] = jnp.zeros_like(dv)

        def group(g, carry):
            for i in range(tiles):

                @pl.when(i < live[b])
                def _():
                    width = (i + 1) * TILE
                    cols = slice(i * TILE, width)
                    q_t = head_rows(qk_t, g, cols)
                    mask = bias[:width, cols]
                    scores = mm(kv[0, g, :width], q_t) + jnp.concatenate([mask] * GROUP, axis=1)
                    prob = jnp.exp(scores - lse[0, g * tiles + i])
                    dp = mm(kv[0, KEY_VALUE_HEADS + g, :width], head_rows(mg_t, g, cols))
                    delta = jnp.sum(prob * dp, axis=0, keepdims=True)
                    ds = (prob * (dp - delta)).astype(bf16)
                    low = prob.astype(bf16)
                    k_t = qk_t[0, pl.ds(MODEL_WIDTH + g * HEAD_SIZE, HEAD_SIZE), :width]
                    dq_i = mm(k_t, ds) * scale
                    for h in range(GROUP):
                        dq[pl.ds((g * GROUP + h) * HEAD_SIZE, HEAD_SIZE), cols] = dq_i[
                            :, h * TILE : (h + 1) * TILE
                        ]
                    q_i = jnp.concatenate([q[g * GROUP + h, cols] for h in range(GROUP)], axis=0)
                    mg_i = jnp.concatenate([mg[g * GROUP + h, cols] for h in range(GROUP)], axis=0)
                    dk[g, :width] += mm(ds, q_i)
                    dv[g, :width] += mm(low, mg_i)

            return carry

        lax.fori_loop(0, KEY_VALUE_HEADS, group, 0)
        c, s = cos[0], sin[0]
        for h in range(QUERY_HEADS + KEY_VALUE_HEADS):
            at = h * HEAD_SIZE
            u = dq[at : at + HEAD_SIZE] if h < QUERY_HEADS else dk[h - QUERY_HEADS].T
            u1, u2 = u[:HALF], u[HALF:]
            r = jnp.concatenate([u1 * c + u2 * s, u2 * c - u1 * s], axis=0)
            low_t[at : at + HEAD_SIZE] = r.astype(bf16)
        for g in range(KEY_VALUE_HEADS):
            at = MODEL_WIDTH + KV_WIDTH + g * HEAD_SIZE
            low_t[at : at + HEAD_SIZE] = dv[g].T.astype(bf16)
        x = tok[0].astype(f32)
        inverse = inverse_rms(x)
        n1 = (x * inverse * gain[...]).astype(bf16)
        dw_t[...] += mm(low_t[...], n1)
        ng = mm(w[...], low_t[...]).T
        dgain[...] += jnp.sum(ng * x * inverse, axis=0, keepdims=True)
        e = ng * gain[...]
        igrad[0] = (
            hgrad[0]
            + inverse * e
            - x * (inverse * inverse * inverse) * jnp.mean(e * x, axis=-1, keepdims=True)
        )


def by_buffer(*shape):
    zeros = (0,) * len(shape)
    return pl.BlockSpec((1,) + shape, lambda b, live: (b,) + zeros)


def whole(*shape):
    zeros = (0,) * len(shape)
    return pl.BlockSpec(shape, lambda b, live: zeros, pipeline_mode=pl.Buffered(1))


def call(kernel, name, buffers, in_specs, out_specs, outs, scratch, flops, moved, args):
    return pl.pallas_call(
        kernel,
        name=name,
        out_shape=[jax.ShapeDtypeStruct(shape, dtype) for shape, dtype in outs],
        grid_spec=pltpu.PrefetchScalarGridSpec(
            num_scalar_prefetch=1,
            grid=(buffers,),
            in_specs=in_specs,
            out_specs=out_specs,
            scratch_shapes=[pltpu.VMEM(shape, dtype) for shape, dtype in scratch],
        ),
        compiler_params=pltpu.CompilerParams(
            dimension_semantics=("arbitrary",), vmem_limit_bytes=60 * 1024 * 1024
        ),
        cost_estimate=pl.CostEstimate(flops=flops, bytes_accessed=moved, transcendentals=0),
    )(*args)


def run_attention_forward(live, tokens, st_row, st_col, cos, sin, wq, wk, wv, wo, gain):
    n, t, d = tokens.shape
    tiles = t // TILE
    return call(
        attention_forward, "attention_forward", n,
        [by_buffer(t, d), by_buffer(1, t), by_buffer(t, 1), by_buffer(HALF, t), by_buffer(HALF, t),
         whole(d, d), whole(d, KV_WIDTH), whole(d, KV_WIDTH), whole(d, d), whole(1, d)],
        [by_buffer(d + KV_WIDTH, t), by_buffer(2 * KEY_VALUE_HEADS, t, HEAD_SIZE), by_buffer(d, t), by_buffer(t, d),
         by_buffer(KEY_VALUE_HEADS * tiles, 1, GROUP * TILE)],
        [((n, d + KV_WIDTH, t), bf16), ((n, 2 * KEY_VALUE_HEADS, t, HEAD_SIZE), bf16), ((n, d, t), bf16), ((n, t, d), f32),
         ((n, KEY_VALUE_HEADS * tiles, 1, GROUP * TILE), f32)],
        [((QKV_WIDTH, d), bf16), ((KEY_VALUE_HEADS, HEAD_SIZE, t), bf16), ((t, t), f32)],
        8 * 10**9, 20 * 10**6,
        (live, tokens, st_row, st_col, cos, sin, wq, wk, wv, wo, gain),
    )


def run_mlp(live, hidden, cot, st_col, wg, wu, wd, gain):
    n, t, d = hidden.shape
    f = FEEDFWD_UNITS
    return call(
        mlp, "mlp", n,
        [by_buffer(t, d), by_buffer(t, d), by_buffer(t, 1), whole(d, f), whole(d, f), whole(f, d), whole(1, d)],
        [by_buffer(t, d), by_buffer(t, d), whole(d, f), whole(d, f), whole(d, f), whole(1, d)],
        [((n, t, d), bf16), ((n, t, d), f32), ((d, f), f32), ((d, f), f32), ((d, f), f32), ((1, d), f32)],
        [((f, d), bf16), ((f, d), bf16), ((d, f), bf16), ((t, d), bf16), ((d, t), bf16), ((t, d), bf16), ((d, t), bf16),
         ((t, d), f32), ((t, d), f32)],
        33 * 10**9, 30 * 10**6,
        (live, hidden, cot, st_col, wg, wu, wd, gain),
    )


def run_attention_backward(live, hgrad, tokens, qk_t, kv, mix_t, lse, st_row, st_col, cos, sin, wq, wk, wv, wo, gain):
    n, t, d = tokens.shape
    tiles = t // TILE
    return call(
        attention_backward, "attention_backward", n,
        [by_buffer(t, d), by_buffer(t, d), by_buffer(d + KV_WIDTH, t), by_buffer(2 * KEY_VALUE_HEADS, t, HEAD_SIZE),
         by_buffer(d, t), by_buffer(KEY_VALUE_HEADS * tiles, 1, GROUP * TILE), by_buffer(1, t), by_buffer(t, 1),
         by_buffer(HALF, t), by_buffer(HALF, t),
         whole(d, d), whole(d, KV_WIDTH), whole(d, KV_WIDTH), whole(d, d), whole(1, d)],
        [by_buffer(t, d), whole(QKV_WIDTH, d), whole(d, d), whole(1, d)],
        [((n, t, d), f32), ((QKV_WIDTH, d), f32), ((d, d), f32), ((1, d), f32)],
        [((d, QKV_WIDTH), bf16), ((t, t), f32), ((1, d, t), bf16), ((QUERY_HEADS, t, HEAD_SIZE), bf16),
         ((QUERY_HEADS, t, HEAD_SIZE), bf16), ((d, t), f32), ((KEY_VALUE_HEADS, t, HEAD_SIZE), f32),
         ((KEY_VALUE_HEADS, t, HEAD_SIZE), f32), ((QKV_WIDTH, t), bf16)],
        16 * 10**9, 40 * 10**6,
        (live, hgrad, tokens, qk_t, kv, mix_t, lse, st_row, st_col, cos, sin, wq, wk, wv, wo, gain),
    )


def unpack(flat_params):
    layout = [
        (MODEL_WIDTH, MODEL_WIDTH),
        (MODEL_WIDTH, KV_WIDTH),
        (MODEL_WIDTH, KV_WIDTH),
        (MODEL_WIDTH, MODEL_WIDTH),
        (MODEL_WIDTH, FEEDFWD_UNITS),
        (MODEL_WIDTH, FEEDFWD_UNITS),
        (FEEDFWD_UNITS, MODEL_WIDTH),
        (2, MODEL_WIDTH),
    ]
    pieces = []
    offset = 0
    for height, breadth in layout:
        pieces.append(flat_params[offset : offset + height * breadth].reshape(height, breadth))
        offset = offset + height * breadth
    return pieces


def local(tokens, doc_starts, cotangent, master, moment_one, moment_two):
    rows = tokens.shape[1]
    whole_rows = master.shape[0] * lax.axis_size("dp")
    flat = lax.all_gather(master.astype(bf16), "dp", axis=0, tiled=True)
    wq, wk, wv, wo, wg, wu, wd, gains = unpack(flat)
    gain_one = gains[0:1].astype(f32)
    gain_two = gains[1:2].astype(f32)

    is_live = doc_starts < rows
    live = jnp.sum(is_live.astype(jnp.int32), axis=1) // TILE
    positions = jnp.where(is_live, jnp.arange(rows) - doc_starts, 0).astype(f32)
    frequency = rope_base ** (-(jnp.arange(HALF, dtype=f32) * 2.0 / HEAD_SIZE))
    angles = frequency[None, :, None] * positions[:, None, :]
    cos, sin = jnp.cos(angles), jnp.sin(angles)
    st_row, st_col = doc_starts[:, None, :], doc_starts[:, :, None]

    qk_t, kv, mix_t, hidden, lse = run_attention_forward(
        live, tokens, st_row, st_col, cos, sin, wq, wk, wv, wo, gain_one
    )
    layer, hgrad, dwg, dwu, dwd_t, dgain_two = run_mlp(live, hidden, cotangent, st_col, wg, wu, wd, gain_two)
    igrad, dw_t, dwo, dgain_one = run_attention_backward(
        live, hgrad, tokens, qk_t, kv, mix_t, lse, st_row, st_col, cos, sin, wq, wk, wv, wo, gain_one
    )
    dw = dw_t.T
    pieces = (
        dw[:, :MODEL_WIDTH], dw[:, MODEL_WIDTH : MODEL_WIDTH + KV_WIDTH], dw[:, MODEL_WIDTH + KV_WIDTH :],
        dwo, dwg, dwu, dwd_t.T, dgain_one, dgain_two,
    )
    flat_grads = jnp.concatenate([piece.reshape(-1) for piece in pieces])
    grads = jnp.pad(flat_grads, (0, whole_rows - flat_grads.shape[0]))
    grad_shard = lax.psum_scatter(grads, "dp", scatter_dimension=0, tiled=True)
    square_sum = lax.psum(jnp.sum(grad_shard * grad_shard), "dp")
    grad_norm = jnp.sqrt(square_sum)
    clipped = grad_shard * (clip_norm / jnp.maximum(grad_norm, clip_norm))
    new_one = decay_one * moment_one + (1.0 - decay_one) * clipped
    new_two = decay_two * moment_two + (1.0 - decay_two) * clipped * clipped
    corrected_one = new_one / (1.0 - decay_one**STEP)
    corrected_two = new_two / (1.0 - decay_two**STEP)
    new_master = master - learn_rate * (
        corrected_one / (jnp.sqrt(corrected_two) + adam_eps) + weight_decay * master
    )
    return (layer, igrad, grad_shard, grad_norm, new_master, new_one, new_two)


def solution(mesh):
    flat, cube = P("dp"), P("dp", None, None)
    return jax.shard_map(
        local,
        mesh=mesh,
        in_specs=(cube, P("dp", None), cube, flat, flat, flat),
        out_specs=(cube, cube, flat, P(), flat, flat, flat),
        check_vma=False,
    )
```

time: 1210 us -> 938 us (0.78)
  matrix products: 365 us -> 0 us
  Pallas kernels: 0 us -> 155 us
  other arithmetic: 230 us -> 159 us
  waiting for transfers between devices: 332 us -> 347 us
    dot_general x124 -> x0, matrix products: 365 us -> none  [the longest x16 101 us: turn_rows(): return jnp.dot(values, turner, precision=lax.Precision.HIGHEST)]
    pallas_call x0 -> x3, Pallas kernels: none -> 155 us  [call(): pl.pallas_call(kernel, name=name, out_shape=[jax.ShapeDtypeStruct(shape,...]
    convert_element_type x13 -> x3, other arithmetic: 50.2 us -> 2.12 us  [the longest x1 1.19 us: local(): flat = lax.all_gather(master.astype(bf16), 'dp', axis=0, tiled=True)]
    unnamed x3, waiting for transfers between devices: 231 us -> 252 us
    unnamed x486 -> x24, local copies, waits for them, and re-layouts: 36.3 us -> 29.7 us
where the time goes in v1:
time: 938 us; the launch traced here: 925 us
  waiting for transfers between devices  347 us (37%)
  local copies, waits for them, and re-layouts  208 us (22%)
  other arithmetic  159 us (17%)
  Pallas kernels  155 us (17%)
  blocking collectives  39.5 us (4%)
  between operations  16.2 us (2%)
    unnamed x3, waiting for transfers between devices  252 us
    pallas_call x3, Pallas kernels, call(): pl.pallas_call(kernel, name=name, out_shape=[jax.ShapeDtypeStruct(shape,...  155 us
    all_gather x1, other arithmetic, local(): flat = lax.all_gather(master.astype(bf16), 'dp', axis=0, tiled=True)  151 us
    concatenate x1, local copies, waits for them, and re-layouts, local(): flat_grads = jnp.concatenate([piece.reshape(-1) for piece in pieces])  104 us
    all_gather x1, waiting for transfers between devices, local(): flat = lax.all_gather(master.astype(bf16), 'dp', axis=0, tiled=True)  95.2 us
    psum x1, blocking collectives, local(): square_sum = lax.psum(jnp.sum(grad_shard * grad_shard), 'dp')  39.5 us
    unnamed x24, local copies, waits for them, and re-layouts  29.7 us
    reshape x7, local copies, waits for them, and re-layouts, local(): flat_grads = jnp.concatenate([piece.reshape(-1) for piece in pieces])  21.7 us
  transfers between devices with their start and end apart: 2, of which 2 were waited for; matrix products, arithmetic and copies ran while one was open for 2% of the time, Pallas kernels for 0%

profile of v1, /device:TPU:0, one launch (start us, length us, event | category | flops | bytes accessed | tf_op | source)
XLA Modules:
  0.0 924.7 jit_solution(5619890150373855324)
XLA Ops:
  7.2 0.0 copy-start.2
  7.2 0.0 all-gather.3.cloned.1.call-start
  7.2 1.2 convert_element_type.23
  8.4 1.0 reshape.94
  9.4 0.0 all-gather.3.cloned.1.call-update
  9.4 0.0 all-reduce.4.cloned.1.call-start
  9.5 1.3 broadcast_in_dim.13.st_row
  10.8 2.1 copy.31.st_col
  12.8 0.0 copy-done.2
  12.8 2.6 copy.30.tok
  15.5 4.3 copy.32.cot
  19.8 0.0 copy-done.6
  19.8 0.1 select_convert_fusion
  19.9 0.5 and_select_fusion.live
  20.5 1.8 multiply_sine_fusion
  22.3 95.2 %all-gather.3.cloned.1.call-done = bf16[32,1,110720]{2,1,0:T(2,128)(2,1)} async-done(((bf16[1,1,110720]{2,1,0:T(2,128)(2,1)}), bf16[32,1,110720]{2,1,0:T(2,128)(2,1)}) %all-gather.3.cloned.1.call-update) | async-done | bytes 7086096 | tf_op jit(solution)/shard_map/all_gather | solution.py:381
  117.5 150.5 %reduce = bf16[32,110720]{1,0:T(8,128)(2,1)} reduce(bf16[32,1,110720]{2,1,0:T(2,128)(2,1)} %all-gather.3.cloned.1.call-done, bf16[]{:T(256)} %constant.57), dimensions={1}, to_apply=%all-gather.reduce_sub_computation | reduce | bytes 14172162 | tf_op jit(solution)/shard_map/all_gather | solution.py:381
  268.0 13.3 %reshape.95 = bf16[3543040]{0:T(1024)(128)(2,1)} reshape(bf16[32,110720]{1,0:T(8,128)(2,1)} %reduce) | data formatting | bytes 14172160
  281.4 2.5 fusion.3
  283.8 1.8 fusion.4
  285.7 0.8 slice_convert_fusion
  286.5 4.1 fusion.2
  290.6 2.3 reshape.76.wq
  292.9 2.6 reshape.79.wo
  295.6 1.9 reshape.77.wk
  297.4 1.9 reshape.78.wv
  299.3 0.6 reshape.92.gain
  299.9 2.8 reshape.82.wd
  302.7 4.4 reshape.80.wg
  307.1 3.0 reshape.81.wu
  310.1 0.6 reshape.93.gain
  310.7 39.3 %attention_forward.1 = (bf16[4,768,512]{2,1,0:T(8,128)(2,1)}, bf16[4,6,512,64]{3,2,1,0:T(8,128)(2,1)}, bf16[4,576,512]{2,1,0:T(8,128)(2,1)}, f32[4,512,576]{2,1,0:T(8,128)}, f32[4,12,1,384]{3,2,1,0:T(1,128)}) custom-call(s32[4]{0:T(128)} %and_select_fusion.live, bf16[4,512,576]{2,1,0:T(8,128)(2,1)} %copy.30.tok, s32[4,1,512]{2,1,0:T(1,128)} %broadcast_in_dim.13.st_row, ...), custom_call_target="tpu_custom_call" | custom-call | flops 8000000000 | bytes 20000000 | tf_op jit(solution)/shard_map/attention_forward/pallas_call | solution.py:290
  350.0 62.3 %mlp.1 = (bf16[4,512,576]{2,1,0:T(8,128)(2,1)}, f32[4,512,576]{2,1,0:T(8,128)}, f32[576,1536]{1,0:T(8,128)}, f32[576,1536]{1,0:T(8,128)}, f32[576,1536]{1,0:T(8,128)}, /*index=5*/f32[1,576]{1,0:T(1,128)}) custom-call(s32[4]{0:T(128)} %and_select_fusion.live, f32[4,512,576]{2,1,0:T(8,128)} %get-tuple-element.22.hidden, bf16[4,512,576]{2,1,0:T(8,128)(2,1)} %copy.32.cot, ...), custom_call_target="tpu_custom_call" | custom-call | flops 32999999488 | bytes 30000000 | tf_op jit(solution)/shard_map/mlp/pallas_call | solution.py:290
  412.4 53.6 %attention_backward.1 = (f32[4,512,576]{2,1,0:T(8,128)}, f32[960,576]{1,0:T(8,128)}, f32[576,576]{1,0:T(8,128)}, f32[1,576]{1,0:T(1,128)}) custom-call(s32[4]{0:T(128)} %and_select_fusion.live, f32[4,512,576]{2,1,0:T(8,128)} %get-tuple-element.24.hgrad, bf16[4,512,576]{2,1,0:T(8,128)(2,1)} %copy.30.tok, bf16[4,768,512]{2,1,0:T(8,128)(2,1)} %get-tuple-element.25.qk_t, ...), custom_call_target="tpu_custom_call" | custom-call | flops 16000000000 | bytes 40000000 | tf_op jit(solution)/shard_map/attention_backward/pallas_call | solution.py:290
  466.0 1.5 slice.62
  467.4 2.0 fusion.5
  469.5 0.5 copy.36
  470.0 1.7 reshape.83
  471.6 1.0 copy.37
  472.7 2.3 reshape.84
  475.0 2.1 copy.38
  477.0 2.1 reshape.85
  479.2 2.8 reshape.86
  481.9 0.0 copy-done
  481.9 3.1 copy.39
  485.0 3.7 reshape.89
  488.7 4.6 reshape.87
  493.3 4.6 reshape.88
  497.9 0.0 copy-done.8
  497.9 0.0 copy-done.7
  497.9 103.8 %concatenate.3 = f32[3540096]{0:T(1024)} concatenate(f32[331776]{0:T(1024)} %reshape.83, f32[110592]{0:T(1024)} %reshape.84, f32[110592]{0:T(1024)} %reshape.85, f32[331776]{0:T(1024)} %reshape.86, f32[884736]{0:T(1024)} %reshape.87, f32[884736]{0:T(1024)} %reshape.88, f32[884736]{0:T(1024)S(1)} %reshape.89, f32[576]{0:T(1024)S(1)} %reduce.1, f32[576]{0:T(1024)S(1)} %reduce.2), dimensions={0} | concatenate | bytes 28320768 | tf_op jit(solution)/shard_map/concatenate | solution.py:406
  601.7 10.5 %pad.4 = f32[3543040]{0:T(1024)} pad(f32[3540096]{0:T(1024)} %concatenate.3, f32[]{:T(128)} %constant.39.clone.1), padding=0_2944 | pad | bytes 28332548 | tf_op jit(solution)/shard_map/jit(_pad)/pad | solution.py:407
  612.2 0.0 all-reduce.4.cloned.1.call-update
  612.3 0.0 copy-start.1
  612.3 5.9 copy.41
  618.1 0.0 copy-done.1
  618.1 2.5 copy.40
  620.7 251.5 %all-reduce.4.cloned.1.call-done = f32[3543040]{0:T(1024)} async-done(((f32[3543040]{0:T(1024)}), f32[3543040]{0:T(1024)}) %all-reduce.4.cloned.1.call-update) | async-done | bytes 14172176
  872.2 1.8 multiply_reduce_fusion
  874.0 39.5 %psum.7 = f32[]{:T(128)} all-reduce(f32[]{:T(128)} %get-tuple-element.61), channel_id=1, replica_groups=mesh['dp'=32] {'dp'}, use_global_device_ids=true, to_apply=%region_3.4 | all-reduce | flops 1 | bytes 8 | tf_op jit(solution)/shard_map/psum | solution.py:409
  914.3 0.0 copy-done.3
  914.3 0.0 copy-done.5
  914.3 2.3 multiply_subtract_fusion
  916.6 0.0 copy-done.4
  (10 shorter events, 0.1 us)
Async XLA Ops:
  7.2 5.7 copy-start.2
  7.2 110.3 %all-gather.3.cloned.1.call-start = ((), (), s32[]{:S(2)}) async-start(), calls=%async_computation | async-start | bytes 14615040 | tf_op jit(solution)/shard_map/all_gather | solution.py:381
  9.4 862.8 %all-reduce.4.cloned.1.call-start = ((), (), s32[]{:S(2)}) async-start(), calls=%async_computation.1 | async-start | bytes 28344320
  15.5 4.4 copy-start.6
  472.7 9.3 %copy-start = (f32[576,1536]{1,0:T(8,128)S(1)}, f32[576,1536]{1,0:T(8,128)}, u32[]{:S(2)}) copy-start(f32[576,1536]{1,0:T(8,128)} %get-tuple-element.34) | copy-start | bytes 10616836
  493.3 4.6 copy-start.8
  493.3 4.6 copy-start.7
  612.3 5.9 copy-start.1
  618.1 296.1 %copy-start.3 = (f32[110720]{0:T(1024)S(1)}, f32[110720]{0:T(1024)}, u32[]{:S(2)}) copy-start(f32[110720]{0:T(1024)} %param.9) | copy-start | bytes 1328644
  618.1 296.1 %copy-start.5 = (f32[110720]{0:T(1024)S(1)}, f32[110720]{0:T(1024)}, u32[]{:S(2)}) copy-start(f32[110720]{0:T(1024)} %param.10) | copy-start | bytes 1328644
  874.0 42.6 %copy-start.4 = (f32[110720]{0:T(1024)}, f32[110720]{0:T(1024)S(1)}, u32[]{:S(2)}) copy-start(f32[110720]{0:T(1024)S(1)} %get-tuple-element.62) | copy-start | bytes 1328644
Sparse Core Ops, SparseCore 0:
  11.5 105.9 all-gather.2
  612.4 259.7 all-reduce.3

commit v2 on v1

--- a/solution.py
+++ b/solution.py
@@ -19,6 +19,10 @@
 KV_WIDTH = KEY_VALUE_HEADS * HEAD_SIZE
 QKV_WIDTH = MODEL_WIDTH + 2 * KV_WIDTH
 CHUNK = 512
+LANES = 128
+UNIT = MODEL_WIDTH * KV_WIDTH // LANES
+GAIN_ROWS = 16
+UNITS = 8
 
 rms_eps = 1e-05
 rope_base = 100000.0
@@ -52,6 +56,48 @@
         bias[:, i * TILE : width] = jnp.where(allowed, 0.0, mask_fill)
 
 
+def half_turn(x):
+    return pltpu.roll(x, HEAD_SIZE, 1)
+
+
+def to_matrix(flat, base, out, pairs, tiles):
+    half = tiles // 2
+    low = lax.broadcasted_iota(jnp.int32, (pairs, LANES), 1) < HEAD_SIZE
+    for t in range(half + 1):
+        out[t, pl.ds(0, pairs, stride=2), :] = flat[pl.ds(base + t, pairs, stride=tiles), :]
+    turned = half_turn(flat[pl.ds(base + half, pairs, stride=tiles), :])
+    for t in range(half):
+        following = half_turn(flat[pl.ds(base + half + t + 1, pairs, stride=tiles), :])
+        out[t, pl.ds(1, pairs, stride=2), :] = jnp.where(low, turned, following)
+        turned = following
+    out[half, pl.ds(1, pairs, stride=2), :] = turned
+
+
+def to_flat(matrix, flat, base, pairs, tiles):
+    half = tiles // 2
+    low = lax.broadcasted_iota(jnp.int32, (pairs, LANES), 1) < HEAD_SIZE
+    for t in range(half):
+        flat[pl.ds(base + t, pairs, stride=tiles), :] = matrix[t, pl.ds(0, pairs, stride=2), :]
+    before = matrix[half, pl.ds(0, pairs, stride=2), :]
+    for t in range(half + 1):
+        turned = half_turn(matrix[t, pl.ds(1, pairs, stride=2), :])
+        flat[pl.ds(base + half + t, pairs, stride=tiles), :] = jnp.where(low, before, turned)
+        before = turned
+
+
+def columns_of(matrix, rows, width):
+    full = width // LANES
+    return jnp.concatenate([matrix[t, :rows] for t in range(full)] + [matrix[full, :rows, :HEAD_SIZE]], axis=1)
+
+
+def put_columns(matrix, value):
+    rows, width = value.shape
+    full = width // LANES
+    for t in range(full):
+        matrix[t, :rows] = value[:, t * LANES : (t + 1) * LANES]
+    matrix[full, :rows, :HEAD_SIZE] = value[:, full * LANES :]
+
+
 def head_rows(ref, g, columns):
     return jnp.concatenate(
         [ref[0, pl.ds((g * GROUP + h) * HEAD_SIZE, HEAD_SIZE), columns] for h in range(GROUP)], axis=1
@@ -59,16 +105,28 @@
 
 
 def attention_forward(
-    live, tok, st_row, st_col, cos, sin, wq, wk, wv, wo, gain, qk_t, kv, mix_t, hidden, lse, w_t, v_t, bias
+    live, own, tok, st_row, st_col, cos, sin, units, gain, qk_t, kv, mix_t, hidden, lse, w, wo, w_t, v_t, bias, flat, square
 ):
     b = pl.program_id(0)
     rows = tok.shape[1]
 
     @pl.when(b == 0)
     def _():
-        w_t[0:MODEL_WIDTH] = wq[...].T
-        w_t[MODEL_WIDTH : MODEL_WIDTH + KV_WIDTH] = wk[...].T
-        w_t[MODEL_WIDTH + KV_WIDTH : QKV_WIDTH] = wv[...].T
+        for k in range(UNITS):
+            flat[k * UNIT : (k + 1) * UNIT] = units[k ^ own[0]].astype(f32)
+        pairs = MODEL_WIDTH // 2
+        to_matrix(flat, 5 * UNIT, square, pairs, 9)
+        wo[...] = columns_of(square, MODEL_WIDTH, MODEL_WIDTH).astype(bf16)
+        to_matrix(flat, 0, square, pairs, 9)
+        value = columns_of(square, MODEL_WIDTH, MODEL_WIDTH)
+        w[:, 0:MODEL_WIDTH] = value.astype(bf16)
+        w_t[0:MODEL_WIDTH] = value.T.astype(bf16)
+        for which in range(2):
+            at = MODEL_WIDTH + which * KV_WIDTH
+            to_matrix(flat, (3 + which) * UNIT, square, pairs, 3)
+            value = columns_of(square, MODEL_WIDTH, KV_WIDTH)
+            w[:, at : at + KV_WIDTH] = value.astype(bf16)
+            w_t[at : at + KV_WIDTH] = value.T.astype(bf16)
 
     @pl.when(live[b] > 0)
     def _():
@@ -122,17 +180,29 @@
 
 
 def mlp(
-    live, hidden, cot, st_col, wg, wu, wd, gain, layer, hgrad, dwg, dwu, dwd_t, dgain,
-    wg_t, wu_t, wd_t, n2, n2_t, rl, rl_t, n2g, res
+    live, own, hidden, cot, st_col, gate_rows, up_rows, down_rows, gain, layer, hgrad, grads, dgain,
+    wg, wu, wd, wg_t, wu_t, wd_t, dwg, dwu, dwd_t, n2, n2_t, rl, rl_t, n2g, res, flat, slab
 ):
     b = pl.program_id(0)
     rows = hidden.shape[1]
 
     @pl.when(b == 0)
     def _():
-        wg_t[...] = wg[...].T
-        wu_t[...] = wu[...].T
-        wd_t[...] = wd[...].T
+        tiles = FEEDFWD_UNITS // LANES
+        for rows_in, straight, turned in ((gate_rows, wg, wg_t), (up_rows, wu, wu_t)):
+            flat[...] = rows_in[...].astype(f32)
+            for j in range(tiles):
+                at = slice(j * LANES, (j + 1) * LANES)
+                part = flat[pl.ds(j, MODEL_WIDTH, stride=tiles), :]
+                straight[:, at] = part.astype(bf16)
+                turned[at] = part.T.astype(bf16)
+        flat[...] = down_rows[...].astype(f32)
+        for j in range(tiles):
+            at = slice(j * LANES, (j + 1) * LANES)
+            to_matrix(flat, j * MODEL_WIDTH, slab, LANES // 2, 9)
+            value = columns_of(slab, LANES, MODEL_WIDTH)
+            wd[at] = value.astype(bf16)
+            wd_t[:, at] = value.T.astype(bf16)
         dwg[...] = jnp.zeros_like(dwg)
         dwu[...] = jnp.zeros_like(dwu)
         dwd_t[...] = jnp.zeros_like(dwd_t)
@@ -186,10 +256,24 @@
             - x * (inverse * inverse * inverse) * jnp.mean(e * x, axis=-1, keepdims=True)
         )
 
+    @pl.when(b == pl.num_programs(0) - 1)
+    def _():
+        tiles = FEEDFWD_UNITS // LANES
+        for p in range(3):
+            for j in range(tiles):
+                at = slice(j * LANES, (j + 1) * LANES)
+                if p < 2:
+                    flat[pl.ds(j, MODEL_WIDTH, stride=tiles), :] = (dwg, dwu)[p][:, at]
+                else:
+                    put_columns(slab, dwd_t[:, at].T)
+                    to_flat(slab, flat, j * MODEL_WIDTH, LANES // 2, 9)
+            for k in range(UNITS):
+                grads[k ^ own[0], p] = flat[k * UNIT : (k + 1) * UNIT].astype(bf16)
+
 
 def attention_backward(
-    live, hgrad, tok, qk_t, kv, mix_t, lse, st_row, st_col, cos, sin, wq, wk, wv, wo, gain,
-    igrad, dw_t, dwo, dgain, w, bias, mg_t, mg, q, dq, dk, dv, low_t
+    live, own, hgrad, tok, qk_t, kv, mix_t, lse, st_row, st_col, cos, sin, w, wo, gain, dgain_two,
+    igrad, grads, dw_t, dwo, dgain, bias, mg_t, mg, q, dq, dk, dv, low_t, flat, square
 ):
     b = pl.program_id(0)
     rows = tok.shape[1]
@@ -198,9 +282,6 @@
 
     @pl.when(b == 0)
     def _():
-        w[:, 0:MODEL_WIDTH] = wq[...]
-        w[:, MODEL_WIDTH : MODEL_WIDTH + KV_WIDTH] = wk[...]
-        w[:, MODEL_WIDTH + KV_WIDTH : QKV_WIDTH] = wv[...]
         dw_t[...] = jnp.zeros_like(dw_t)
         dwo[...] = jnp.zeros_like(dwo)
         dgain[...] = jnp.zeros_like(dgain)
@@ -275,15 +356,40 @@
             - x * (inverse * inverse * inverse) * jnp.mean(e * x, axis=-1, keepdims=True)
         )
 
+    @pl.when(b == pl.num_programs(0) - 1)
+    def _():
+        pairs = MODEL_WIDTH // 2
+        put_columns(square, dw_t[0:MODEL_WIDTH].T)
+        to_flat(square, flat, 0, pairs, 9)
+        for which in range(2):
+            at = MODEL_WIDTH + which * KV_WIDTH
+            put_columns(square, dw_t[at : at + KV_WIDTH].T)
+            to_flat(square, flat, (3 + which) * UNIT, pairs, 3)
+        put_columns(square, dwo[...])
+        to_flat(square, flat, 5 * UNIT, pairs, 9)
+        gains = jnp.concatenate([dgain[...], dgain_two[...]], axis=1)
+        gains = jnp.concatenate([gains[:, j * LANES : (j + 1) * LANES] for j in range(9)], axis=0)
+        for k in range(UNITS):
+            grads[k ^ own[0], 0:UNIT] = flat[k * UNIT : (k + 1) * UNIT].astype(bf16)
+            grads[k, UNIT : UNIT + GAIN_ROWS] = jnp.zeros((GAIN_ROWS, LANES), bf16)
+        at = (UNITS - 1) ^ own[0]
+        grads[at, UNIT : UNIT + GAIN_ROWS] = jnp.concatenate(
+            [gains, jnp.zeros((GAIN_ROWS - 9, LANES), f32)], axis=0
+        ).astype(bf16)
+
 
 def by_buffer(*shape):
     zeros = (0,) * len(shape)
-    return pl.BlockSpec((1,) + shape, lambda b, live: (b,) + zeros)
+    return pl.BlockSpec((1,) + shape, lambda b, live, own: (b,) + zeros)
 
 
 def whole(*shape):
     zeros = (0,) * len(shape)
-    return pl.BlockSpec(shape, lambda b, live: zeros, pipeline_mode=pl.Buffered(1))
+    return pl.BlockSpec(shape, lambda b, live, own: zeros, pipeline_mode=pl.Buffered(1))
+
+
+def quarter(which):
+    return pl.BlockSpec((UNITS * UNIT, LANES), lambda b, live, own: (which, 0), pipeline_mode=pl.Buffered(1))
 
 
 def call(kernel, name, buffers, in_specs, out_specs, outs, scratch, flops, moved, args):
@@ -292,7 +398,7 @@
         name=name,
         out_shape=[jax.ShapeDtypeStruct(shape, dtype) for shape, dtype in outs],
         grid_spec=pltpu.PrefetchScalarGridSpec(
-            num_scalar_prefetch=1,
+            num_scalar_prefetch=2,
             grid=(buffers,),
             in_specs=in_specs,
             out_specs=out_specs,
@@ -305,83 +411,130 @@
     )(*args)
 
 
-def run_attention_forward(live, tokens, st_row, st_col, cos, sin, wq, wk, wv, wo, gain):
+def run_attention_forward(live, own, tokens, st_row, st_col, cos, sin, units, gain):
     n, t, d = tokens.shape
     tiles = t // TILE
     return call(
         attention_forward, "attention_forward", n,
         [by_buffer(t, d), by_buffer(1, t), by_buffer(t, 1), by_buffer(HALF, t), by_buffer(HALF, t),
-         whole(d, d), whole(d, KV_WIDTH), whole(d, KV_WIDTH), whole(d, d), whole(1, d)],
+         whole(UNITS, UNIT, LANES), whole(1, d)],
         [by_buffer(d + KV_WIDTH, t), by_buffer(2 * KEY_VALUE_HEADS, t, HEAD_SIZE), by_buffer(d, t), by_buffer(t, d),
-         by_buffer(KEY_VALUE_HEADS * tiles, 1, GROUP * TILE)],
+         by_buffer(KEY_VALUE_HEADS * tiles, 1, GROUP * TILE), whole(d, QKV_WIDTH), whole(d, d)],
         [((n, d + KV_WIDTH, t), bf16), ((n, 2 * KEY_VALUE_HEADS, t, HEAD_SIZE), bf16), ((n, d, t), bf16), ((n, t, d), f32),
-         ((n, KEY_VALUE_HEADS * tiles, 1, GROUP * TILE), f32)],
-        [((QKV_WIDTH, d), bf16), ((KEY_VALUE_HEADS, HEAD_SIZE, t), bf16), ((t, t), f32)],
+         ((n, KEY_VALUE_HEADS * tiles, 1, GROUP * TILE), f32), ((d, QKV_WIDTH), bf16), ((d, d), bf16)],
+        [((QKV_WIDTH, d), bf16), ((KEY_VALUE_HEADS, HEAD_SIZE, t), bf16), ((t, t), f32), ((UNITS * UNIT, LANES), f32),
+         ((5, d, LANES), f32)],
         8 * 10**9, 20 * 10**6,
-        (live, tokens, st_row, st_col, cos, sin, wq, wk, wv, wo, gain),
-    )
-
-
-def run_mlp(live, hidden, cot, st_col, wg, wu, wd, gain):
+        (live, own, tokens, st_row, st_col, cos, sin, units, gain),
+    )
+
+
+def run_mlp(live, own, hidden, cot, st_col, rows, gain):
     n, t, d = hidden.shape
     f = FEEDFWD_UNITS
     return call(
         mlp, "mlp", n,
-        [by_buffer(t, d), by_buffer(t, d), by_buffer(t, 1), whole(d, f), whole(d, f), whole(f, d), whole(1, d)],
-        [by_buffer(t, d), by_buffer(t, d), whole(d, f), whole(d, f), whole(d, f), whole(1, d)],
-        [((n, t, d), bf16), ((n, t, d), f32), ((d, f), f32), ((d, f), f32), ((d, f), f32), ((1, d), f32)],
-        [((f, d), bf16), ((f, d), bf16), ((d, f), bf16), ((t, d), bf16), ((d, t), bf16), ((t, d), bf16), ((d, t), bf16),
-         ((t, d), f32), ((t, d), f32)],
+        [by_buffer(t, d), by_buffer(t, d), by_buffer(t, 1), quarter(1), quarter(2), quarter(3), whole(1, d)],
+        [by_buffer(t, d), by_buffer(t, d), whole(UNITS, 3, UNIT, LANES), whole(1, d)],
+        [((n, t, d), bf16), ((n, t, d), f32), ((UNITS, 3, UNIT, LANES), bf16), ((1, d), f32)],
+        [((d, f), bf16), ((d, f), bf16), ((f, d), bf16), ((f, d), bf16), ((f, d), bf16), ((d, f), bf16),
+         ((d, f), f32), ((d, f), f32), ((d, f), f32), ((t, d), bf16), ((d, t), bf16), ((t, d), bf16), ((d, t), bf16),
+         ((t, d), f32), ((t, d), f32), ((UNITS * UNIT, LANES), f32), ((5, LANES, LANES), f32)],
         33 * 10**9, 30 * 10**6,
-        (live, hidden, cot, st_col, wg, wu, wd, gain),
-    )
-
-
-def run_attention_backward(live, hgrad, tokens, qk_t, kv, mix_t, lse, st_row, st_col, cos, sin, wq, wk, wv, wo, gain):
+        (live, own, hidden, cot, st_col, rows, rows, rows, gain),
+    )
+
+
+def run_attention_backward(live, own, hgrad, tokens, qk_t, kv, mix_t, lse, st_row, st_col, cos, sin, w, wo, gain, dgain_two):
     n, t, d = tokens.shape
     tiles = t // TILE
     return call(
         attention_backward, "attention_backward", n,
         [by_buffer(t, d), by_buffer(t, d), by_buffer(d + KV_WIDTH, t), by_buffer(2 * KEY_VALUE_HEADS, t, HEAD_SIZE),
          by_buffer(d, t), by_buffer(KEY_VALUE_HEADS * tiles, 1, GROUP * TILE), by_buffer(1, t), by_buffer(t, 1),
-         by_buffer(HALF, t), by_buffer(HALF, t),
-         whole(d, d), whole(d, KV_WIDTH), whole(d, KV_WIDTH), whole(d, d), whole(1, d)],
-        [by_buffer(t, d), whole(QKV_WIDTH, d), whole(d, d), whole(1, d)],
-        [((n, t, d), f32), ((QKV_WIDTH, d), f32), ((d, d), f32), ((1, d), f32)],
-        [((d, QKV_WIDTH), bf16), ((t, t), f32), ((1, d, t), bf16), ((QUERY_HEADS, t, HEAD_SIZE), bf16),
-         ((QUERY_HEADS, t, HEAD_SIZE), bf16), ((d, t), f32), ((KEY_VALUE_HEADS, t, HEAD_SIZE), f32),
-         ((KEY_VALUE_HEADS, t, HEAD_SIZE), f32), ((QKV_WIDTH, t), bf16)],
+         by_buffer(HALF, t), by_buffer(HALF, t), whole(d, QKV_WIDTH), whole(d, d), whole(1, d), whole(1, d)],
+        [by_buffer(t, d), whole(UNITS, UNIT + GAIN_ROWS, LANES)],
+        [((n, t, d), f32), ((UNITS, UNIT + GAIN_ROWS, LANES), bf16)],
+        [((QKV_WIDTH, d), f32), ((d, d), f32), ((1, d), f32), ((t, t), f32), ((1, d, t), bf16),
+         ((QUERY_HEADS, t, HEAD_SIZE), bf16), ((QUERY_HEADS, t, HEAD_SIZE), bf16), ((d, t), f32),
+         ((KEY_VALUE_HEADS, t, HEAD_SIZE), f32), ((KEY_VALUE_HEADS, t, HEAD_SIZE), f32), ((QKV_WIDTH, t), bf16),
+         ((UNITS * UNIT, LANES), f32), ((5, d, LANES), f32)],
         16 * 10**9, 40 * 10**6,
-        (live, hgrad, tokens, qk_t, kv, mix_t, lse, st_row, st_col, cos, sin, wq, wk, wv, wo, gain),
-    )
-
-
-def unpack(flat_params):
-    layout = [
-        (MODEL_WIDTH, MODEL_WIDTH),
-        (MODEL_WIDTH, KV_WIDTH),
-        (MODEL_WIDTH, KV_WIDTH),
-        (MODEL_WIDTH, MODEL_WIDTH),
-        (MODEL_WIDTH, FEEDFWD_UNITS),
-        (MODEL_WIDTH, FEEDFWD_UNITS),
-        (FEEDFWD_UNITS, MODEL_WIDTH),
-        (2, MODEL_WIDTH),
-    ]
-    pieces = []
-    offset = 0
-    for height, breadth in layout:
-        pieces.append(flat_params[offset : offset + height * breadth].reshape(height, breadth))
-        offset = offset + height * breadth
-    return pieces
+        (live, own, hgrad, tokens, qk_t, kv, mix_t, lse, st_row, st_col, cos, sin, w, wo, gain, dgain_two),
+    )
+
+
+def swap(x, bits):
+    size = lax.axis_size("dp")
+    return lax.ppermute(x, "dp", [(i, i ^ bits) for i in range(size)])
+
+
+def plane(i):
+    return i // UNITS
+
+
+def relative_order(unit):
+    z = plane(lax.axis_index("dp"))
+    first = jnp.where(z == 0, unit, jnp.zeros_like(unit))
+    for far in (3, 2, 1):
+        first = first + lax.ppermute(unit, "dp", [(k, far * UNITS + k) for k in range(UNITS)])
+    even = [first, swap(first, 2), swap(first, 4), swap(first, 6)]
+    units = []
+    for piece in even:
+        units += [piece, swap(piece, 1)]
+    return jnp.stack(units)
+
+
+def spread_last(rows):
+    size = lax.axis_size("dp")
+    have = [size - 1]
+    me = lax.axis_index("dp")
+    rows = jnp.where(me == size - 1, rows, jnp.zeros_like(rows))
+    bits = 1
+    while bits < size:
+        rows = rows + lax.ppermute(rows, "dp", [(i, i ^ bits) for i in have])
+        have = have + [i ^ bits for i in have]
+        bits *= 2
+    return rows
+
+
+def reduce_in_plane(grads):
+    other = swap(grads[1::2], 1)
+    both = grads[0::2].astype(f32) + other.astype(f32)
+    low = both.astype(bf16)
+    return ((both[0] + swap(low[1], 2).astype(f32)) + (swap(low[2], 4).astype(f32) + swap(low[3], 6).astype(f32)))
+
+
+def add_up(value):
+    value = value + swap(value, 1)
+    value = (value + swap(value, 2)) + (swap(value, 4) + swap(value, 6))
+    return (value + swap(value, 8)) + (swap(value, 16) + swap(value, 24))
 
 
 def local(tokens, doc_starts, cotangent, master, moment_one, moment_two):
+    size = lax.axis_size("dp")
+    me = lax.axis_index("dp")
     rows = tokens.shape[1]
-    whole_rows = master.shape[0] * lax.axis_size("dp")
-    flat = lax.all_gather(master.astype(bf16), "dp", axis=0, tiled=True)
-    wq, wk, wv, wo, wg, wu, wd, gains = unpack(flat)
-    gain_one = gains[0:1].astype(f32)
-    gain_two = gains[1:2].astype(f32)
+    shard = master.shape[0] // LANES
+    total = 4 * UNITS * UNIT
+    by_units = size == 4 * UNITS and shard == UNIT + 1
+    own_rows = master.reshape(shard, LANES)
+    if by_units:
+        own = me % UNITS
+        before = lax.ppermute(own_rows[shard - size :], "dp", [(i, i + 1) for i in range(size - 1)])
+        unit = lax.dynamic_slice_in_dim(jnp.concatenate([before, own_rows], axis=0), size - me, UNIT).astype(bf16)
+        gain_at = total - (size - 1) * shard
+        gain_rows = spread_last(own_rows[gain_at : gain_at + GAIN_ROWS].astype(bf16))
+        units = relative_order(unit)
+        all_rows = lax.all_gather(unit, "dp", axis=0, tiled=True)
+    else:
+        own = jnp.zeros_like(me)
+        all_rows = lax.all_gather(own_rows.astype(bf16), "dp", axis=0, tiled=True)
+        gain_rows = all_rows[total : total + GAIN_ROWS]
+        units = all_rows[: UNITS * UNIT].reshape(UNITS, UNIT, LANES)
+    gains = gain_rows.reshape(-1)[: 2 * MODEL_WIDTH].reshape(2, MODEL_WIDTH).astype(f32)
+    gain_one, gain_two = gains[0:1], gains[1:2]
+    own = own.astype(jnp.int32).reshape(1)
 
     is_live = doc_starts < rows
     live = jnp.sum(is_live.astype(jnp.int32), axis=1) // TILE
@@ -391,22 +544,44 @@
     cos, sin = jnp.cos(angles), jnp.sin(angles)
     st_row, st_col = doc_starts[:, None, :], doc_starts[:, :, None]
 
-    qk_t, kv, mix_t, hidden, lse = run_attention_forward(
-        live, tokens, st_row, st_col, cos, sin, wq, wk, wv, wo, gain_one
-    )
-    layer, hgrad, dwg, dwu, dwd_t, dgain_two = run_mlp(live, hidden, cotangent, st_col, wg, wu, wd, gain_two)
-    igrad, dw_t, dwo, dgain_one = run_attention_backward(
-        live, hgrad, tokens, qk_t, kv, mix_t, lse, st_row, st_col, cos, sin, wq, wk, wv, wo, gain_one
-    )
-    dw = dw_t.T
-    pieces = (
-        dw[:, :MODEL_WIDTH], dw[:, MODEL_WIDTH : MODEL_WIDTH + KV_WIDTH], dw[:, MODEL_WIDTH + KV_WIDTH :],
-        dwo, dwg, dwu, dwd_t.T, dgain_one, dgain_two,
-    )
-    flat_grads = jnp.concatenate([piece.reshape(-1) for piece in pieces])
-    grads = jnp.pad(flat_grads, (0, whole_rows - flat_grads.shape[0]))
-    grad_shard = lax.psum_scatter(grads, "dp", scatter_dimension=0, tiled=True)
-    square_sum = lax.psum(jnp.sum(grad_shard * grad_shard), "dp")
+    qk_t, kv, mix_t, hidden, lse, w, wo = run_attention_forward(
+        live, own, tokens, st_row, st_col, cos, sin, units, gain_one
+    )
+    layer, hgrad, late, dgain_two = run_mlp(live, own, hidden, cotangent, st_col, all_rows, gain_two)
+    igrad, early = run_attention_backward(
+        live, own, hgrad, tokens, qk_t, kv, mix_t, lse, st_row, st_col, cos, sin, w, wo, gain_one, dgain_two
+    )
+    if by_units:
+        z = plane(me)
+        last = size // UNITS - 1
+        late_sum = reduce_in_plane(late)
+        mine = lax.dynamic_index_in_dim(late_sum, jnp.maximum(z - 1, 0), 0, keepdims=False)
+        for far in (1, 2, 3):
+            to = z ^ far
+            sent = lax.dynamic_index_in_dim(late_sum, jnp.maximum(to - 1, 0), 0, keepdims=False).astype(bf16)
+            pairs = [(i, i ^ (far * UNITS)) for i in range(size) if plane(i ^ (far * UNITS)) > 0]
+            mine = mine + lax.ppermute(sent, "dp", pairs).astype(f32)
+        early_sum = reduce_in_plane(early)
+        early_low = early_sum.astype(bf16)
+        first = early_sum[:UNIT]
+        gain_grads = early_sum[UNIT:]
+        for far in (1, 2, 3):
+            sent = lax.ppermute(early_low[:UNIT], "dp", [(far * UNITS + k, k) for k in range(UNITS)])
+            first = first + sent.astype(f32)
+            top = [((last ^ far) * UNITS + k, last * UNITS + k) for k in range(UNITS)]
+            gain_grads = gain_grads + lax.ppermute(early_low[UNIT:], "dp", top).astype(f32)
+        unit_grad = jnp.where(z == 0, first, mine)
+        gain_grads = jnp.where(me == size - 1, gain_grads, 0.0)
+        square_sum = add_up((jnp.sum(unit_grad * unit_grad) + jnp.sum(gain_grads * gain_grads)).reshape(1, 1))[0, 0]
+        after = lax.ppermute(unit_grad[:size], "dp", [(i + 1, i) for i in range(size - 1)])
+        after = after + jnp.pad(gain_grads, ((0, size - GAIN_ROWS), (0, 0)))
+        grad_shard = lax.dynamic_slice_in_dim(jnp.concatenate([unit_grad, after], axis=0), me, shard).reshape(-1)
+    else:
+        pieces = [early[:, :UNIT].reshape(-1, LANES)] + [late[:, p].reshape(-1, LANES) for p in range(3)]
+        grads = jnp.concatenate(pieces + [early[UNITS - 1, UNIT:]], axis=0).astype(f32)
+        grads = jnp.pad(grads, ((0, size * shard - grads.shape[0]), (0, 0)))
+        grad_shard = lax.psum_scatter(grads.reshape(-1), "dp", scatter_dimension=0, tiled=True)
+        square_sum = lax.psum(jnp.sum(grad_shard * grad_shard), "dp")
     grad_norm = jnp.sqrt(square_sum)
     clipped = grad_shard * (clip_norm / jnp.maximum(grad_norm, clip_norm))
     new_one = decay_one * moment_one + (1.0 - decay_one) * clipped

time: 938 us -> 389 us (0.41); the launches traced: 925 us -> 386 us
  waiting for transfers between devices: 347 us -> 76.9 us
  local copies, waits for them, and re-layouts: 208 us -> 32.4 us
  other arithmetic: 159 us -> 20.9 us
  starting transfers between devices: 0.08 us -> 107 us
  blocking collectives: 39.5 us -> 0 us
  Pallas kernels: 155 us -> 127 us
    unnamed x3 -> x1, waiting for transfers between devices: 252 us -> 0.02 us
    all_gather x1 -> x0, other arithmetic: 151 us -> none  [local(): flat = lax.all_gather(master.astype(bf16), 'dp', axis=0, tiled=True)]
    ppermute x0 -> x41, starting transfers between devices: none -> 107 us  [the longest x22 56.4 us: swap(): return lax.ppermute(x, 'dp', [(i, i ^ bits) for i in range(size)])]
    concatenate x1 -> x0, local copies, waits for them, and re-layouts: 104 us -> none  [local(): flat_grads = jnp.concatenate([piece.reshape(-1) for piece in pieces])]
    all_gather x1, waiting for transfers between devices: 95.2 us -> 0.02 us  [local(): all_rows = lax.all_gather(unit, 'dp', axis=0, tiled=True)]
    ppermute x0 -> x41, waiting for transfers between devices: none -> 76.9 us  [the longest x22 59.7 us: swap(): return lax.ppermute(x, 'dp', [(i, i ^ bits) for i in range(size)])]
    reshape x14 -> x0, local copies, waits for them, and re-layouts: 40.6 us -> none  [the longest x7 21.7 us: local(): flat_grads = jnp.concatenate([piece.reshape(-1) for piece in pieces])]
    psum x1 -> x0, blocking collectives: 39.5 us -> none  [local(): square_sum = lax.psum(jnp.sum(grad_shard * grad_shard), 'dp')]
  transfers between devices with their start and end apart: 2 -> 42, of which waited for: 2 -> 13; matrix products, arithmetic and copies ran while one was open for 2% -> 11% of each run, Pallas kernels for 0% -> 19%
where the time goes in v2:
time: 389 us; the launch traced here: 386 us
  Pallas kernels  127 us (33%)
  starting transfers between devices  107 us (28%)
  waiting for transfers between devices  76.9 us (20%)
  local copies, waits for them, and re-layouts  32.4 us (8%)
  between operations  21.5 us (6%)
  other arithmetic  20.9 us (5%)
    pallas_call x3, Pallas kernels, call(): pl.pallas_call(kernel, name=name, out_shape=[jax.ShapeDtypeStruct(shape,...  127 us
    ppermute x22, waiting for transfers between devices, swap(): return lax.ppermute(x, 'dp', [(i, i ^ bits) for i in range(size)])  59.7 us
    ppermute x22, starting transfers between devices, swap(): return lax.ppermute(x, 'dp', [(i, i ^ bits) for i in range(size)])  56.4 us
    ppermute x3, starting transfers between devices, relative_order(): lax.ppermute(unit, 'dp', [(k, far * UNITS + k) for k in range(UNITS)])  21 us
    unnamed x30, local copies, waits for them, and re-layouts  19.8 us
    ppermute x3, starting transfers between devices, local(): mine = mine + lax.ppermute(sent, 'dp', pairs).astype(f32)  15.2 us
    ppermute x3, waiting for transfers between devices, relative_order(): lax.ppermute(unit, 'dp', [(k, far * UNITS + k) for k in range(UNITS)])  14.9 us
  transfers between devices with their start and end apart: 42, of which 13 were waited for; matrix products, arithmetic and copies ran while one was open for 11% of the time, Pallas kernels for 19%

profile of v2, /device:TPU:0, one launch (start us, length us, event | category | flops | bytes accessed | tf_op | source)
XLA Modules:
  0.0 385.9 jit_solution(5147228745940141587)
XLA Ops:
  7.2 0.9 slice_bitcast_fusion.8
  8.1 2.3 collective-permute-start
  10.5 0.8 collective-permute-done
  11.3 1.8 fusion.8
  15.9 0.8 select_convert_fusion
  18.8 1.8 multiply_sine_fusion
  20.6 1.3 collective-permute-start.15
  22.4 1.3 broadcast_in_dim.23.st_row
  23.7 2.0 copy.19.st_col
  25.8 2.6 copy.18.tok
  28.4 4.4 %copy.20.cot = bf16[4,512,576]{2,1,0:T(8,128)(2,1)} copy(bf16[4,512,576]{1,2,0:T(8,128)(2,1)} %param.8) | data formatting | bytes 4718592 | tf_op args[2]
  32.7 18.4 %collective-permute-start.1 = (bf16[864,128]{1,0:T(8,128)(2,1)S(1)}, bf16[864,128]{1,0:T(8,128)(2,1)S(1)}, u32[]{:S(2)}, u32[]{:S(2)}) collective-permute-start(bf16[864,128]{1,0:T(8,128)(2,1)S(1)} %copy-done.2), channel_id=1, source_target_pairs={{0,24},{1,25},{2,26},{3,27},{4,28},{5,29},{6,30},{7,31}} | collective-permute-start | bytes 663560 | tf_op jit(solution)/shard_map/ppermute | solution.py:480
  51.1 1.3 collective-permute-start.2
  52.4 1.3 collective-permute-start.3
  53.8 6.7 %collective-permute-done.1 = bf16[864,128]{1,0:T(8,128)(2,1)S(1)} collective-permute-done((bf16[864,128]{1,0:T(8,128)(2,1)S(1)}, bf16[864,128]{1,0:T(8,128)(2,1)S(1)}, u32[]{:S(2)}, u32[]{:S(2)}) %collective-permute-start.1) | collective-permute-done | bytes 221216 | tf_op jit(solution)/shard_map/ppermute | solution.py:480
  60.5 4.7 %collective-permute-done.2 = bf16[864,128]{1,0:T(8,128)(2,1)S(1)} collective-permute-done((bf16[864,128]{1,0:T(8,128)(2,1)S(1)}, bf16[864,128]{1,0:T(8,128)(2,1)S(1)}, u32[]{:S(2)}, u32[]{:S(2)}) %collective-permute-start.2) | collective-permute-done | bytes 221216 | tf_op jit(solution)/shard_map/ppermute | solution.py:480
  65.3 3.5 collective-permute-done.3
  69.0 1.1 collective-permute-start.5
  70.0 0.9 collective-permute-start.7
  70.9 1.6 collective-permute-start.9
  73.1 8.6 %collective-permute-done.5 = bf16[864,128]{1,0:T(8,128)(2,1)S(1)} collective-permute-done((bf16[864,128]{1,0:T(8,128)(2,1)S(1)}, bf16[864,128]{1,0:T(8,128)(2,1)S(1)}, u32[]{:S(2)}, u32[]{:S(2)}) %collective-permute-start.5) | collective-permute-done | bytes 221216 | tf_op jit(solution)/shard_map/ppermute | solution.py:469
  81.7 2.2 collective-permute-done.7
  83.9 7.2 %collective-permute-done.9 = bf16[864,128]{1,0:T(8,128)(2,1)S(1)} collective-permute-done((bf16[864,128]{1,0:T(8,128)(2,1)S(1)}, bf16[864,128]{1,0:T(8,128)(2,1)S(1)}, u32[]{:S(2)}, u32[]{:S(2)}) %collective-permute-start.9) | collective-permute-done | bytes 221216 | tf_op jit(solution)/shard_map/ppermute | solution.py:469
  91.3 1.2 collective-permute-done.10
  92.5 1.2 copy-done.9
  93.8 35.2 %attention_forward.1 = (bf16[4,768,512]{2,1,0:T(8,128)(2,1)}, bf16[4,6,512,64]{3,2,1,0:T(8,128)(2,1)}, bf16[4,576,512]{2,1,0:T(8,128)(2,1)}, f32[4,512,576]{2,1,...) custom-call(s32[4]{0:T(128)} %and_select_fusion.live, s32[1]{0:T(128)} %bitcast.own, ...), custom_call_target="tpu_custom_call" | custom-call | flops 8000000000 | bytes 20000000 | tf_op jit(solution)/shard_map/attention_forward/pallas_call | solution.py:396
  129.0 53.1 %mlp.1 = (bf16[4,512,576]{2,1,0:T(8,128)(2,1)}, f32[4,512,576]{2,1,0:T(8,128)}, bf16[8,3,864,128]{3,2,1,0:T(8,128)(2,1)}, f32[1,576]{1,0:T(1,128)}) custom-call(s32[4]{0:T(128)} %and_select_fusion.live, s32[1]{0:T(128)} %bitcast.own, f32[4,512,576]{2,1,0:T(8,128)} %get-tuple-element.20.hidden, bf16[4,512,576]{2,1,0:T(8,128)(2,1)} %copy.20.cot, ...), custom_call_target="tpu_custom_call" | custom-call | flops 32999999488 | bytes 30000000 | tf_op jit(solution)/shard_map/mlp/pallas_call | solution.py:396
  182.1 3.4 slice.107
  185.5 3.7 collective-permute-start.23
  189.2 38.5 %attention_backward.1 = (f32[4,512,576]{2,1,0:T(8,128)}, bf16[8,880,128]{2,1,0:T(8,128)(2,1)}) custom-call(s32[4]{0:T(128)} %and_select_fusion.live, s32[1]{0:T(128)} %bitcast.own, f32[4,512,576]{2,1,0:T(8,128)} %get-tuple-element.22.hgrad, bf16[4,512,576]{2,1,0:T(8,128)(2,1)} %copy.18.tok, bf16[4,768,512]{2,1,0:T(8,128)(2,1)} %get-tuple-element.23.qk_t, ...), custom_call_target="tpu_custom_call" | custom-call | flops 16000000000 | bytes 40000000 | tf_op jit(solution)/shard_map/attention_backward/pallas_call | solution.py:396
  227.7 1.4 slice.99
  229.1 4.9 %collective-permute-start.16 = (bf16[4,880,128]{2,1,0:T(8,128)(2,1)S(1)}, bf16[4,880,128]{2,1,0:T(8,128)(2,1)S(1)}, u32[]{:S(2)}, u32[]{:S(2)}) collective-permute-start(bf16[4,880,128]{2,1,0:T(8,128)(2,1)S(1)} %slice.99), channel_id=1, source_target_pairs={{0,1},{1,0},{2,3},{3,2},{4,5},{5,4},{6,7},{7,6},{8,9},{9,8},{10,11... | collective-permute-start | bytes 2703368 | tf_op jit(solution)/shard_map/ppermute | solution.py:469
  233.9 2.1 collective-permute-done.16
  237.0 17.8 %collective-permute-start.17 = (bf16[880,128]{1,0:T(8,128)(2,1)S(1)}, bf16[880,128]{1,0:T(8,128)(2,1)S(1)}, u32[]{:S(2)}, u32[]{:S(2)}) collective-permute-start(bf16[880,128]{1,0:T(8,128)(2,1)S(1)} %get-tuple-element.69), channel_id=1, source_target_pairs={{0,2},{1,3},{2,0},{3,1},{4,6},{5,7},{6,4},{7,5},{8,10},{9,11},{10,... | collective-permute-start | bytes 675848 | tf_op jit(solution)/shard_map/ppermute | solution.py:469
  254.8 5.0 %fusion.24 = (bf16[4,3,864,128]{3,2,1,0:T(8,128)(2,1)S(1)}, f32[4,3,864,128]{3,2,1,0:T(8,128)}) fusion(bf16[4,3,864,128]{3,2,1,0:T(8,128)(2,1)} %collective-permute-done.23, bf16[8,3,864,128]{3,2,1,0:T(8,128)(2,1)S(1)} %copy-done), kind=kLoop, calls=%fused_computation.72 | loop fusion | flops 5308416 | bytes 13271040 | tf_op jit(solution)/shard_map/convert_element_type | solution.py:504
  259.8 1.3 slice_bitcast_fusion.3
  261.1 1.6 collective-permute-start.24
  262.7 1.9 collective-permute-start.26
  264.8 2.9 collective-permute-start.19
  267.7 36.0 %collective-permute-done.18 = bf16[880,128]{1,0:T(8,128)(2,1)S(1)} collective-permute-done((bf16[880,128]{1,0:T(8,128)(2,1)}, bf16[880,128]{1,0:T(8,128)(2,1)S(1)}, u32[]{:S(2)}, u32[]{:S(2)}) %collective-permute-start.18) | collective-permute-done | bytes 225312 | tf_op jit(solution)/shard_map/ppermute | solution.py:469
  305.1 1.2 fusion.29
  306.3 1.3 collective-permute-start.20
  307.6 1.3 collective-permute-start.21
  308.9 1.3 collective-permute-start.22
  310.2 2.0 fusion.1
  312.2 0.9 fusion.14
  313.0 8.2 %collective-permute-start.27 = (bf16[864,128]{1,0:T(8,128)(2,1)}, bf16[864,128]{1,0:T(8,128)(2,1)}, u32[]{:S(2)}, u32[]{:S(2)}) collective-permute-start(bf16[864,128]{1,0:T(8,128)(2,1)} %get-tuple-element.66), channel_id=1, source_target_pairs={{0,8},{1,9},{2,10},{3,11},{4,12},{5,13},{6,14},{7,15},{16,24},{17,... | collective-permute-start | bytes 663560 | tf_op jit(solution)/shard_map/ppermute | solution.py:563
  321.2 5.0 %collective-permute-start.28 = (bf16[864,128]{1,0:T(8,128)(2,1)}, bf16[864,128]{1,0:T(8,128)(2,1)}, u32[]{:S(2)}, u32[]{:S(2)}) collective-permute-start(bf16[864,128]{1,0:T(8,128)(2,1)} %get-tuple-element.68), channel_id=1, source_target_pairs={{0,16},{1,17},{2,18},{3,19},{4,20},{5,21},{6,22},{7,23},{8,24},{9,... | collective-permute-start | bytes 663560 | tf_op jit(solution)/shard_map/ppermute | solution.py:563
  326.2 1.4 collective-permute-done.20
  327.6 2.0 collective-permute-start.29
  329.6 5.7 %copy.25 = f32[4,512,576]{1,2,0:T(8,128)} copy(f32[4,512,576]{2,1,0:T(8,128)} %get-tuple-element.41) | data formatting | bytes 9437184
  335.3 4.3 %copy.24 = bf16[4,512,576]{1,2,0:T(8,128)(2,1)} copy(bf16[4,512,576]{2,1,0:T(8,128)(2,1)} %get-tuple-element.40) | data formatting | bytes 4718592
  341.1 1.9 collective-permute-start.33
  343.0 2.2 multiply_reduce_fusion
  345.3 1.3 collective-permute-start.30
  348.5 2.1 collective-permute-start.34
  351.2 2.2 collective-permute-start.36
  353.4 2.2 collective-permute-start.37
  355.6 3.0 collective-permute-start.35
  361.1 7.1 %collective-permute-start.39 = (f32[1,1]{1,0:T(1,128)}, f32[1,1]{1,0:T(1,128)}, u32[]{:S(2)}, u32[]{:S(2)}) collective-permute-start(f32[1,1]{1,0:T(1,128)} %add.174), channel_id=1, source_target_pairs={{0,16},{1,17},{2,18},{3,19},{4,20},{5,21},{6,22},{7,23},{8,24},{9,... | collective-permute-start | bytes 20 | tf_op jit(solution)/shard_map/ppermute | solution.py:469
  368.2 1.7 collective-permute-start.40
  369.9 1.4 collective-permute-start.38
  371.3 2.1 collective-permute-done.38
  375.5 2.5 multiply_subtract_fusion
  (88 shorter events, 11.6 us)
Async XLA Ops:
  7.2 18.6 %copy-start.1 = (bf16[4,512,576]{1,2,0:T(8,128)(2,1)S(1)}, bf16[4,512,576]{1,2,0:T(8,128)(2,1)}, u32[]{:S(2)}) copy-start(bf16[4,512,576]{1,2,0:T(8,128)(2,1)} %param.6) | copy-start | bytes 7077892
  7.2 121.8 %all-gather.2.cloned.1.call-start = ((), (), s32[]{:S(2)}) async-start(), calls=%async_computation | async-start | bytes 7299072 | tf_op jit(solution)/shard_map/all_gather | solution.py:529
  8.1 3.2 collective-permute-start
  13.8 0.7 collective-permute-start.11
  15.2 1.5 collective-permute-start.12
  17.4 0.7 collective-permute-start.13
  18.1 2.5 collective-permute-start.14
  20.6 33.1 %collective-permute-start.15 = (bf16[16,128]{1,0:T(8,128)(2,1)S(1)}, bf16[16,128]{1,0:T(8,128)(2,1)S(1)}, u32[]{:S(2)}, u32[]{:S(2)}) collective-permute-start(bf16[16,128]{1,0:T(8,128)(2,1)S(1)} %add.149), channel_id=1, source_target_pairs={{31,15},{30,14},{29,13},{28,12},{27,11},{26,10},{25,9},{24,8},{23,... | collective-permute-start | bytes 12296 | tf_op jit(solution)/shard_map/ppermute | solution.py:495
  28.4 4.4 %copy-start.2 = (bf16[864,128]{1,0:T(8,128)(2,1)S(1)}, bf16[864,128]{1,0:T(8,128)(2,1)}, u32[]{:S(2)}) copy-start(bf16[864,128]{1,0:T(8,128)(2,1)} %fusion.8) | copy-start | bytes 663556
  32.7 27.8 %collective-permute-start.1 = (bf16[864,128]{1,0:T(8,128)(2,1)S(1)}, bf16[864,128]{1,0:T(8,128)(2,1)S(1)}, u32[]{:S(2)}, u32[]{:S(2)}) collective-permute-start(bf16[864,128]{1,0:T(8,128)(2,1)S(1)} %copy-done.2), channel_id=1, source_target_pairs={{0,24},{1,25},{2,26},{3,27},{4,28},{5,29},{6,30},{7,31}} | collective-permute-start | bytes 663560 | tf_op jit(solution)/shard_map/ppermute | solution.py:480
  51.1 14.1 %collective-permute-start.2 = (bf16[864,128]{1,0:T(8,128)(2,1)S(1)}, bf16[864,128]{1,0:T(8,128)(2,1)S(1)}, u32[]{:S(2)}, u32[]{:S(2)}) collective-permute-start(bf16[864,128]{1,0:T(8,128)(2,1)S(1)} %copy-done.2), channel_id=1, source_target_pairs={{0,16},{1,17},{2,18},{3,19},{4,20},{5,21},{6,22},{7,23}} | collective-permute-start | bytes 663560 | tf_op jit(solution)/shard_map/ppermute | solution.py:480
  52.4 16.3 %collective-permute-start.3 = (bf16[864,128]{1,0:T(8,128)(2,1)S(1)}, bf16[864,128]{1,0:T(8,128)(2,1)S(1)}, u32[]{:S(2)}, u32[]{:S(2)}) collective-permute-start(bf16[864,128]{1,0:T(8,128)(2,1)S(1)} %copy-done.2), channel_id=1, source_target_pairs={{0,8},{1,9},{2,10},{3,11},{4,12},{5,13},{6,14},{7,15}} | collective-permute-start | bytes 663560 | tf_op jit(solution)/shard_map/ppermute | solution.py:480
  68.9 22.1 %collective-permute-start.4 = (bf16[864,128]{1,0:T(8,128)(2,1)S(1)}, bf16[864,128]{1,0:T(8,128)(2,1)S(1)}, u32[]{:S(2)}, u32[]{:S(2)}) collective-permute-start(bf16[864,128]{1,0:T(8,128)(2,1)S(1)} %get-tuple-element.58), channel_id=1, source_target_pairs={{0,1},{1,0},{2,3},{3,2},{4,5},{5,4},{6,7},{7,6},{8,9},{9,8},{10,11... | collective-permute-start | bytes 663560 | tf_op jit(solution)/shard_map/ppermute | solution.py:469
  69.0 12.7 %collective-permute-start.5 = (bf16[864,128]{1,0:T(8,128)(2,1)S(1)}, bf16[864,128]{1,0:T(8,128)(2,1)S(1)}, u32[]{:S(2)}, u32[]{:S(2)}) collective-permute-start(bf16[864,128]{1,0:T(8,128)(2,1)S(1)} %get-tuple-element.58), channel_id=1, source_target_pairs={{0,2},{1,3},{2,0},{3,1},{4,6},{5,7},{6,4},{7,5},{8,10},{9,11},{10,... | collective-permute-start | bytes 663560 | tf_op jit(solution)/shard_map/ppermute | solution.py:469
  70.0 13.8 %collective-permute-start.7 = (bf16[864,128]{1,0:T(8,128)(2,1)S(1)}, bf16[864,128]{1,0:T(8,128)(2,1)S(1)}, u32[]{:S(2)}, u32[]{:S(2)}) collective-permute-start(bf16[864,128]{1,0:T(8,128)(2,1)S(1)} %get-tuple-element.58), channel_id=1, source_target_pairs={{0,4},{1,5},{2,6},{3,7},{4,0},{5,1},{6,2},{7,3},{8,12},{9,13},{10,... | collective-permute-start | bytes 663560 | tf_op jit(solution)/shard_map/ppermute | solution.py:469
  70.9 20.1 %collective-permute-start.9 = (bf16[864,128]{1,0:T(8,128)(2,1)S(1)}, bf16[864,128]{1,0:T(8,128)(2,1)S(1)}, u32[]{:S(2)}, u32[]{:S(2)}) collective-permute-start(bf16[864,128]{1,0:T(8,128)(2,1)S(1)} %get-tuple-element.58), channel_id=1, source_target_pairs={{0,6},{1,7},{2,4},{3,5},{4,2},{5,3},{6,0},{7,1},{8,14},{9,15},{10,... | collective-permute-start | bytes 663560 | tf_op jit(solution)/shard_map/ppermute | solution.py:469
  81.7 9.4 %collective-permute-start.6 = (bf16[864,128]{1,0:T(8,128)(2,1)S(1)}, bf16[864,128]{1,0:T(8,128)(2,1)S(1)}, u32[]{:S(2)}, u32[]{:S(2)}) collective-permute-start(bf16[864,128]{1,0:T(8,128)(2,1)S(1)} %collective-permute-done.5), channel_id=1, source_target_pairs={{0,1},{1,0},{2,3},{3,2},{4,5},{5,4},{6,7},{7,6},{8,9},{9,8},{10,11... | collective-permute-start | bytes 663560 | tf_op jit(solution)/shard_map/ppermute | solution.py:469
  83.8 7.3 %collective-permute-start.8 = (bf16[864,128]{1,0:T(8,128)(2,1)S(1)}, bf16[864,128]{1,0:T(8,128)(2,1)S(1)}, u32[]{:S(2)}, u32[]{:S(2)}) collective-permute-start(bf16[864,128]{1,0:T(8,128)(2,1)S(1)} %collective-permute-done.7), channel_id=1, source_target_pairs={{0,1},{1,0},{2,3},{3,2},{4,5},{5,4},{6,7},{7,6},{8,9},{9,8},{10,11... | collective-permute-start | bytes 663560 | tf_op jit(solution)/shard_map/ppermute | solution.py:469
  91.0 1.5 collective-permute-start.10
  92.5 1.2 copy-start.9
  185.5 69.4 %collective-permute-start.23 = (bf16[4,3,864,128]{3,2,1,0:T(8,128)(2,1)}, bf16[4,3,864,128]{3,2,1,0:T(8,128)(2,1)}, u32[]{:S(2)}, u32[]{:S(2)}) collective-permute-start(bf16[4,3,864,128]{3,2,1,0:T(8,128)(2,1)} %slice.107), channel_id=1, source_target_pairs={{0,1},{1,0},{2,3},{3,2},{4,5},{5,4},{6,7},{7,6},{8,9},{9,8},{10,11... | collective-permute-start | bytes 7962632 | tf_op jit(solution)/shard_map/ppermute | solution.py:469
  227.7 8.3 %copy-start.4 = (bf16[8,880,128]{2,1,0:T(8,128)(2,1)S(1)}, bf16[8,880,128]{2,1,0:T(8,128)(2,1)}, u32[]{:S(2)}) copy-start(bf16[8,880,128]{2,1,0:T(8,128)(2,1)} %get-tuple-element.31) | copy-start | bytes 5406724
  229.1 6.9 %collective-permute-start.16 = (bf16[4,880,128]{2,1,0:T(8,128)(2,1)S(1)}, bf16[4,880,128]{2,1,0:T(8,128)(2,1)S(1)}, u32[]{:S(2)}, u32[]{:S(2)}) collective-permute-start(bf16[4,880,128]{2,1,0:T(8,128)(2,1)S(1)} %slice.99), channel_id=1, source_target_pairs={{0,1},{1,0},{2,3},{3,2},{4,5},{5,4},{6,7},{7,6},{8,9},{9,8},{10,11... | collective-permute-start | bytes 2703368 | tf_op jit(solution)/shard_map/ppermute | solution.py:469
  236.0 18.8 %copy-start = (bf16[8,3,864,128]{3,2,1,0:T(8,128)(2,1)S(1)}, bf16[8,3,864,128]{3,2,1,0:T(8,128)(2,1)}, u32[]{:S(2)}) copy-start(bf16[8,3,864,128]{3,2,1,0:T(8,128)(2,1)} %get-tuple-element.32) | copy-start | bytes 15925252
  237.0 27.8 %collective-permute-start.17 = (bf16[880,128]{1,0:T(8,128)(2,1)S(1)}, bf16[880,128]{1,0:T(8,128)(2,1)S(1)}, u32[]{:S(2)}, u32[]{:S(2)}) collective-permute-start(bf16[880,128]{1,0:T(8,128)(2,1)S(1)} %get-tuple-element.69), channel_id=1, source_target_pairs={{0,2},{1,3},{2,0},{3,1},{4,6},{5,7},{6,4},{7,5},{8,10},{9,11},{10,... | collective-permute-start | bytes 675848 | tf_op jit(solution)/shard_map/ppermute | solution.py:469
  261.1 47.7 %collective-permute-start.24 = (bf16[3,864,128]{2,1,0:T(8,128)(2,1)}, bf16[3,864,128]{2,1,0:T(8,128)(2,1)S(1)}, u32[]{:S(2)}, u32[]{:S(2)}) collective-permute-start(bf16[3,864,128]{2,1,0:T(8,128)(2,1)} %get-tuple-element.63), channel_id=1, source_target_pairs={{0,2},{1,3},{2,0},{3,1},{4,6},{5,7},{6,4},{7,5},{8,10},{9,11},{10,... | collective-permute-start | bytes 1990664 | tf_op jit(solution)/shard_map/ppermute | solution.py:469
  262.7 47.4 %collective-permute-start.25 = (bf16[3,864,128]{2,1,0:T(8,128)(2,1)}, bf16[3,864,128]{2,1,0:T(8,128)(2,1)}, u32[]{:S(2)}, u32[]{:S(2)}) collective-permute-start(bf16[3,864,128]{2,1,0:T(8,128)(2,1)} %get-tuple-element.65), channel_id=1, source_target_pairs={{0,4},{1,5},{2,6},{3,7},{4,0},{5,1},{6,2},{7,3},{8,12},{9,13},{10,... | collective-permute-start | bytes 1990664 | tf_op jit(solution)/shard_map/ppermute | solution.py:469
  262.7 47.4 %collective-permute-start.26 = (bf16[3,864,128]{2,1,0:T(8,128)(2,1)}, bf16[3,864,128]{2,1,0:T(8,128)(2,1)}, u32[]{:S(2)}, u32[]{:S(2)}) collective-permute-start(bf16[3,864,128]{2,1,0:T(8,128)(2,1)} %get-tuple-element.64), channel_id=1, source_target_pairs={{0,6},{1,7},{2,4},{3,5},{4,2},{5,3},{6,0},{7,1},{8,14},{9,15},{10,... | collective-permute-start | bytes 1990664 | tf_op jit(solution)/shard_map/ppermute | solution.py:469
  264.6 39.1 %collective-permute-start.18 = (bf16[880,128]{1,0:T(8,128)(2,1)}, bf16[880,128]{1,0:T(8,128)(2,1)S(1)}, u32[]{:S(2)}, u32[]{:S(2)}) collective-permute-start(bf16[880,128]{1,0:T(8,128)(2,1)} %get-tuple-element.71), channel_id=1, source_target_pairs={{0,4},{1,5},{2,6},{3,7},{4,0},{5,1},{6,2},{7,3},{8,12},{9,13},{10,... | collective-permute-start | bytes 675848 | tf_op jit(solution)/shard_map/ppermute | solution.py:469
  264.8 38.9 %collective-permute-start.19 = (bf16[880,128]{1,0:T(8,128)(2,1)S(1)}, bf16[880,128]{1,0:T(8,128)(2,1)S(1)}, u32[]{:S(2)}, u32[]{:S(2)}) collective-permute-start(bf16[880,128]{1,0:T(8,128)(2,1)S(1)} %get-tuple-element.70), channel_id=1, source_target_pairs={{0,6},{1,7},{2,4},{3,5},{4,2},{5,3},{6,0},{7,1},{8,14},{9,15},{10,... | collective-permute-start | bytes 675848 | tf_op jit(solution)/shard_map/ppermute | solution.py:469
  303.7 0.7 copy-start.6
  304.4 0.7 copy-start.7
  306.3 21.4 %collective-permute-start.20 = (bf16[864,128]{1,0:T(8,128)(2,1)S(1)}, bf16[864,128]{1,0:T(8,128)(2,1)S(1)}, u32[]{:S(2)}, u32[]{:S(2)}) collective-permute-start(bf16[864,128]{1,0:T(8,128)(2,1)S(1)} %slice.125), channel_id=1, source_target_pairs={{8,0},{9,1},{10,2},{11,3},{12,4},{13,5},{14,6},{15,7}} | collective-permute-start | bytes 663560 | tf_op jit(solution)/shard_map/ppermute | solution.py:569
  307.6 32.1 %collective-permute-start.21 = (bf16[864,128]{1,0:T(8,128)(2,1)S(1)}, bf16[864,128]{1,0:T(8,128)(2,1)}, u32[]{:S(2)}, u32[]{:S(2)}) collective-permute-start(bf16[864,128]{1,0:T(8,128)(2,1)S(1)} %slice.125), channel_id=1, source_target_pairs={{16,0},{17,1},{18,2},{19,3},{20,4},{21,5},{22,6},{23,7}} | collective-permute-start | bytes 663560 | tf_op jit(solution)/shard_map/ppermute | solution.py:569
  308.9 31.6 %collective-permute-start.22 = (bf16[864,128]{1,0:T(8,128)(2,1)S(1)}, bf16[864,128]{1,0:T(8,128)(2,1)}, u32[]{:S(2)}, u32[]{:S(2)}) collective-permute-start(bf16[864,128]{1,0:T(8,128)(2,1)S(1)} %slice.125), channel_id=1, source_target_pairs={{24,0},{25,1},{26,2},{27,3},{28,4},{29,5},{30,6},{31,7}} | collective-permute-start | bytes 663560 | tf_op jit(solution)/shard_map/ppermute | solution.py:569
  313.0 28.1 %collective-permute-start.27 = (bf16[864,128]{1,0:T(8,128)(2,1)}, bf16[864,128]{1,0:T(8,128)(2,1)}, u32[]{:S(2)}, u32[]{:S(2)}) collective-permute-start(bf16[864,128]{1,0:T(8,128)(2,1)} %get-tuple-element.66), channel_id=1, source_target_pairs={{0,8},{1,9},{2,10},{3,11},{4,12},{5,13},{6,14},{7,15},{16,24},{17,... | collective-permute-start | bytes 663560 | tf_op jit(solution)/shard_map/ppermute | solution.py:563
  321.2 21.8 %collective-permute-start.28 = (bf16[864,128]{1,0:T(8,128)(2,1)}, bf16[864,128]{1,0:T(8,128)(2,1)}, u32[]{:S(2)}, u32[]{:S(2)}) collective-permute-start(bf16[864,128]{1,0:T(8,128)(2,1)} %get-tuple-element.68), channel_id=1, source_target_pairs={{0,16},{1,17},{2,18},{3,19},{4,20},{5,21},{6,22},{7,23},{8,24},{9,... | collective-permute-start | bytes 663560 | tf_op jit(solution)/shard_map/ppermute | solution.py:563
  327.6 7.7 %copy-start.8 = (bf16[864,128]{1,0:T(8,128)(2,1)}, bf16[864,128]{1,0:T(8,128)(2,1)S(1)}, u32[]{:S(2)}) copy-start(bf16[864,128]{1,0:T(8,128)(2,1)S(1)} %collective-permute-done.20) | copy-start | bytes 663556
  327.6 15.4 %collective-permute-start.29 = (bf16[864,128]{1,0:T(8,128)(2,1)}, bf16[864,128]{1,0:T(8,128)(2,1)}, u32[]{:S(2)}, u32[]{:S(2)}) collective-permute-start(bf16[864,128]{1,0:T(8,128)(2,1)} %get-tuple-element.67), channel_id=1, source_target_pairs={{0,24},{1,25},{2,26},{3,27},{4,28},{5,29},{6,30},{7,31},{8,16},{9,... | collective-permute-start | bytes 663560 | tf_op jit(solution)/shard_map/ppermute | solution.py:563
  339.6 35.9 %copy-start.3 = (f32[110720]{0:T(1024)S(1)}, f32[110720]{0:T(1024)}, u32[]{:S(2)}) copy-start(f32[110720]{0:T(1024)} %param.9) | copy-start | bytes 1328644
  339.6 35.9 %copy-start.5 = (f32[110720]{0:T(1024)S(1)}, f32[110720]{0:T(1024)}, u32[]{:S(2)}) copy-start(f32[110720]{0:T(1024)} %param.10) | copy-start | bytes 1328644
  339.6 6.9 %collective-permute-start.31 = (bf16[16,128]{1,0:T(8,128)(2,1)S(1)}, bf16[16,128]{1,0:T(8,128)(2,1)S(1)}, u32[]{:S(2)}, u32[]{:S(2)}) collective-permute-start(bf16[16,128]{1,0:T(8,128)(2,1)S(1)} %slice.132), channel_id=1, source_target_pairs={{16,24},{17,25},{18,26},{19,27},{20,28},{21,29},{22,30},{23,31}} | collective-permute-start | bytes 12296 | tf_op jit(solution)/shard_map/ppermute | solution.py:572
  340.4 6.1 %collective-permute-start.32 = (bf16[16,128]{1,0:T(8,128)(2,1)S(1)}, bf16[16,128]{1,0:T(8,128)(2,1)S(1)}, u32[]{:S(2)}, u32[]{:S(2)}) collective-permute-start(bf16[16,128]{1,0:T(8,128)(2,1)S(1)} %slice.132), channel_id=1, source_target_pairs={{8,24},{9,25},{10,26},{11,27},{12,28},{13,29},{14,30},{15,31}} | collective-permute-start | bytes 12296 | tf_op jit(solution)/shard_map/ppermute | solution.py:572
  341.1 5.5 %collective-permute-start.33 = (bf16[16,128]{1,0:T(8,128)(2,1)S(1)}, bf16[16,128]{1,0:T(8,128)(2,1)S(1)}, u32[]{:S(2)}, u32[]{:S(2)}) collective-permute-start(bf16[16,128]{1,0:T(8,128)(2,1)S(1)} %slice.132), channel_id=1, source_target_pairs={{0,24},{1,25},{2,26},{3,27},{4,28},{5,29},{6,30},{7,31}} | collective-permute-start | bytes 12296 | tf_op jit(solution)/shard_map/ppermute | solution.py:572
  345.3 30.2 %collective-permute-start.30 = (f32[32,128]{1,0:T(8,128)S(1)}, f32[32,128]{1,0:T(8,128)S(1)}, u32[]{:S(2)}, u32[]{:S(2)}) collective-permute-start(f32[32,128]{1,0:T(8,128)S(1)} %slice.130), channel_id=1, source_target_pairs={{1,0},{2,1},{3,2},{4,3},{5,4},{6,5},{7,6},{8,7},{9,8},{10,9},{11,1... | collective-permute-start | bytes 49160 | tf_op jit(solution)/shard_map/ppermute | solution.py:576
  348.5 2.1 collective-permute-start.34
  351.2 8.6 %collective-permute-start.36 = (f32[1,1]{1,0:T(1,128)}, f32[1,1]{1,0:T(1,128)}, u32[]{:S(2)}, u32[]{:S(2)}) collective-permute-start(f32[1,1]{1,0:T(1,128)} %add.171), channel_id=1, source_target_pairs={{0,4},{1,5},{2,6},{3,7},{4,0},{5,1},{6,2},{7,3},{8,12},{9,13},{10,... | collective-permute-start | bytes 20 | tf_op jit(solution)/shard_map/ppermute | solution.py:469
  353.4 6.4 %collective-permute-start.37 = (f32[1,1]{1,0:T(1,128)}, f32[1,1]{1,0:T(1,128)}, u32[]{:S(2)}, u32[]{:S(2)}) collective-permute-start(f32[1,1]{1,0:T(1,128)} %add.171), channel_id=1, source_target_pairs={{0,6},{1,7},{2,4},{3,5},{4,2},{5,3},{6,0},{7,1},{8,14},{9,15},{10,... | collective-permute-start | bytes 20 | tf_op jit(solution)/shard_map/ppermute | solution.py:469
  355.6 3.5 collective-permute-start.35
  361.1 13.0 %collective-permute-start.39 = (f32[1,1]{1,0:T(1,128)}, f32[1,1]{1,0:T(1,128)}, u32[]{:S(2)}, u32[]{:S(2)}) collective-permute-start(f32[1,1]{1,0:T(1,128)} %add.174), channel_id=1, source_target_pairs={{0,16},{1,17},{2,18},{3,19},{4,20},{5,21},{6,22},{7,23},{8,24},{9,... | collective-permute-start | bytes 20 | tf_op jit(solution)/shard_map/ppermute | solution.py:469
  368.2 5.9 %collective-permute-start.40 = (f32[1,1]{1,0:T(1,128)}, f32[1,1]{1,0:T(1,128)}, u32[]{:S(2)}, u32[]{:S(2)}) collective-permute-start(f32[1,1]{1,0:T(1,128)} %add.174), channel_id=1, source_target_pairs={{0,24},{1,25},{2,26},{3,27},{4,28},{5,29},{6,30},{7,31},{8,16},{9,... | collective-permute-start | bytes 20 | tf_op jit(solution)/shard_map/ppermute | solution.py:469
  369.9 3.5 collective-permute-start.38
Sparse Core Ops, SparseCore 0:
  13.2 91.4 all-gather.1
